TPU v7x, 256 devices: a whole 4x4x8 slice. The times are simulated.
256 devices in a mesh: seq: 16 (over y, x), head: 16 (over z, core).
Axes of the slice: x: 4, y: 4, z: 8, core: 2. Of those that a mesh axis runs over, the one named last changes fastest.
Arguments:
- queries: bfloat16 [8192, 2048], P('seq', 'head'), may hold values from -5 to 5
- keys: bfloat16 [8192, 2048], P('seq', 'head'), may hold values from -5 to 5
- values: bfloat16 [8192, 2048], P('seq', 'head'), may hold values from -5 to 5
- grad_out: bfloat16 [8192, 2048], P('seq', 'head'), may hold values from -6 to 6
Outputs:
- attended: bfloat16 [8192, 2048], P('seq', 'head')
- grad_query: bfloat16 [8192, 2048], P(('seq', 'head'))
- grad_key: bfloat16 [8192, 2048], P(('seq', 'head'))
- grad_value: bfloat16 [8192, 2048], P(('seq', 'head'))
All inputs are finite; a program needn't handle non-finite values.
Results may differ from a plain program's by a relative error of at most 0.024.
Values may be sent and summed in bfloat16 or wider, within the bound.
A program may use at most 64 MiB of HBM per device.

v0:
```python
import functools

import jax
import jax.numpy as jnp
from jax import lax
from jax.experimental import pallas as pl
from jax.experimental.pallas import tpu as pltpu
from jax.sharding import PartitionSpec as P

BLOCK = 128
WIDE = 256
NEG = -1e30
F32 = jnp.float32
BF16 = jnp.bfloat16
LOG2E = 1.4426950408889634
MESH = pl.DeviceIdType.MESH
OFF = (0, 512, 768, 896, 960)
STACK = 992
SEM = (0, 2, 4, 7, 13)
SLOTS = 21
ROWS = (128, 256, 128, 64, 32)
SLOT_COUNT = (2, 2, 3, 6, 8)

NN = (((1,), (0,)), ((), ()))
NT = (((1,), (1,)), ((), ()))
TN = (((0,), (0,)), ((), ()))


def dot(a, b, dims=NN):
    return lax.dot_general(a, b, dims, preferred_element_type=F32)


def halve(x):
    n, w = x.shape
    x = x.reshape(n // 16, 2, 8, w)
    m = (x[:, 0] + x[:, 1]) * 0.5
    return m.astype(BF16).astype(F32).reshape(n // 2, w)


def expand(x, level):
    n, w = x.shape
    if level == 0:
        return x
    x = x.reshape(n // 8, 1, 8, w)
    x = jnp.broadcast_to(x, (n // 8, 1 << level, 8, w))
    return x.reshape(n << level, w)


def group(x, level):
    n, w = x.shape
    if level == 0:
        return x
    return x.reshape(n >> (level + 3), 1 << level, 8, w).sum(axis=1).reshape(n >> level, w)


def peers_of(s, seq_count):
    out = []
    prev, after = lax.rem(s + seq_count - 1, seq_count), lax.rem(s + 1, seq_count)
    a, e = lax.div(s, 2), lax.rem(s, 2)
    y, x = lax.div(s, 4), lax.rem(s, 4)

    def third(i, n):
        return lax.rem(i + n + 3 - 6 * lax.rem(i, 2), n)

    blocks = seq_count // 2
    for f in range(4):
        out.append((4, lax.rem(y + 2, 4) * 4 + f, f, x))
    for f in range(4):
        out.append((4, (3 - y) * 4 + f, 4 + f, 4 + x))
    far3 = third(a, blocks)
    for f in range(2):
        out.append((3, far3 * 2 + f, 4 + f, 4 + e))
    for f in range(2):
        out.append((3, lax.rem(a + blocks - 2, blocks) * 2 + f, f, 2 + e))
        out.append((3, lax.rem(a + 2, blocks) * 2 + f, 2 + f, e))
    out.append((2, third(s, seq_count), 2, 2))
    out.append((2, lax.rem(s + seq_count - 2, seq_count), 0, 1))
    out.append((2, lax.rem(s + 2, seq_count), 1, 0))
    out.append((1, prev, 0, 1))
    out.append((1, after, 1, 0))
    out.append((0, prev, 0, 1))
    out.append((0, after, 1, 0))
    return out


def kernel(
    seq_count, head_count,
    q_ref, k_ref, v_ref, g_ref,
    att_ref, gq_ref, gk_ref, gv_ref,
    kv0, kv1, kv2, kv3, kv4, in1, in2, in3, in4,
    qs, go, ee, pk, tot, sm, gg, dd, dq,
    acc0, acc1, bk0, bk1, bk2, bk3, bk4, rx0, rx1, rx2, rx3, rx4,
    oq, ok, ov,
    send_sem, recv_sem, back_send, back_recv, out_send, out_recv,
):
    s, h = lax.axis_index("seq"), lax.axis_index("head")
    barrier = pltpu.get_barrier_semaphore()
    for j in range(1, seq_count):
        pl.semaphore_signal(
            barrier, inc=1, device_id={"seq": lax.rem(s + j, seq_count)}, device_id_type=MESH
        )
    for j in range(1, head_count):
        pl.semaphore_signal(
            barrier, inc=1, device_id={"head": lax.rem(h + j, head_count)}, device_id_type=MESH
        )

    row = lax.broadcasted_iota(jnp.int32, (BLOCK, BLOCK), 0)
    col = lax.broadcasted_iota(jnp.int32, (BLOCK, BLOCK), 1)
    perm = jnp.where(col == (row & 7) * 16 + (row >> 3), 1.0, 0.0).astype(BF16)
    unperm = jnp.where(col == (row & 15) * 8 + (row >> 4), 1.0, 0.0).astype(BF16)

    own = (kv0, kv1, kv2, kv3, kv4)
    tops = []
    for b in range(4):
        rows = pl.ds(BLOCK * b, BLOCK)
        fine = dot(perm, jnp.concatenate([k_ref[rows, :], v_ref[rows, :]], axis=1))
        kv0[pl.ds(BLOCK + BLOCK * b, BLOCK), :] = fine.astype(BF16)
        m1 = halve(fine)
        kv1[pl.ds(64 * ((b + 2) % 4), 64), :] = m1.astype(BF16)
        m2 = halve(m1)
        kv2[pl.ds(32 * b, 32), :] = m2.astype(BF16)
        m3 = halve(m2)
        kv3[pl.ds(16 * b, 16), :] = m3.astype(BF16)
        tops.append(halve(m3))
    kv4[...] = jnp.concatenate(tops, axis=0).astype(BF16)

    pl.semaphore_wait(barrier, seq_count - 1 + head_count - 1)

    peers = peers_of(s, seq_count)
    inbox = (kv0, in1, in2, in3, in4)
    outbox = (bk0, bk1, bk2, bk3, bk4)
    rxbox = (rx0, rx1, rx2, rx3, rx4)

    def at_slot(ref, level, slot, spread=False):
        n = ROWS[level]
        if spread:
            return ref.at[pl.ds(640 * slot, n), :]
        return ref.at[pl.ds(n * slot, n), :]

    def forward_copy(entry):
        level, peer, slot, there = entry
        if level == 0:
            src = kv0.at[pl.ds(BLOCK + 384 * slot, BLOCK), :]
        else:
            src = own[level]
        return pltpu.make_async_remote_copy(
            src_ref=src,
            dst_ref=at_slot(inbox[level], level, there, level == 0),
            send_sem=send_sem.at[SEM[level] + slot],
            recv_sem=recv_sem.at[SEM[level] + there],
            device_id={"seq": peer},
            device_id_type=MESH,
        )

    def forward_arrival(level, slot):
        here = at_slot(inbox[level], level, slot, level == 0)
        pltpu.make_async_remote_copy(
            src_ref=here, dst_ref=here,
            send_sem=send_sem.at[SEM[level] + slot], recv_sem=recv_sem.at[SEM[level] + slot],
            device_id={"seq": s}, device_id_type=MESH,
        ).wait_recv()

    def back_copy(entry):
        level, peer, slot, there = entry
        return pltpu.make_async_remote_copy(
            src_ref=at_slot(outbox[level], level, slot),
            dst_ref=at_slot(rxbox[level], level, there),
            send_sem=back_send.at[SEM[level] + slot],
            recv_sem=back_recv.at[SEM[level] + there],
            device_id={"seq": peer},
            device_id_type=MESH,
        )

    def back_arrival(level, slot):
        here = at_slot(rxbox[level], level, slot)
        pltpu.make_async_remote_copy(
            src_ref=here, dst_ref=here,
            send_sem=back_send.at[SEM[level] + slot], recv_sem=back_recv.at[SEM[level] + slot],
            device_id={"seq": s}, device_id_type=MESH,
        ).wait_recv()

    for entry in peers:
        forward_copy(entry).start()

    tops = []
    for b in range(4):
        rows = pl.ds(BLOCK * b, BLOCK)
        both = dot(perm, jnp.concatenate([q_ref[rows, :], g_ref[rows, :]], axis=1))
        go[rows, :] = both[:, BLOCK:]
        fine = both[:, :BLOCK]
        qs[rows, :] = fine.astype(BF16)
        m1 = halve(fine)
        qs[pl.ds(OFF[1] + 64 * b, 64), :] = m1.astype(BF16)
        m2 = halve(m1)
        qs[pl.ds(OFF[2] + 32 * b, 32), :] = m2.astype(BF16)
        m3 = halve(m2)
        qs[pl.ds(OFF[3] + 16 * b, 16), :] = m3.astype(BF16)
        tops.append(halve(m3))
    qs[pl.ds(OFF[4], 32), :] = jnp.concatenate(tops, axis=0).astype(BF16)

    scale = BLOCK ** (-0.5)
    lane = lax.broadcasted_iota(jnp.int32, (8, 384), 1)

    def off_if(bad):
        return jnp.where(bad, NEG, 0.0).astype(F32)

    no_prev, no_next = off_if(s == 0), off_if(s == seq_count - 1)
    a, y = lax.div(s, 2), lax.div(s, 4)

    def thirds(first, second, last):
        return jnp.where(lane < 128, first, jnp.where(lane < 256, second, last))[:1]

    def slot_bias(i, n):
        even = lax.rem(i, 2) == 0
        return thirds(
            off_if(i < 2), off_if(i + 2 > n - 1),
            off_if((even & (i + 3 > n - 1)) | (jnp.logical_not(even) & (i < 3))),
        )

    bias1 = (
        thirds(no_prev, no_next, no_next),
        thirds(no_prev, no_prev, no_next),
    )
    bias2 = slot_bias(s, seq_count)
    bias3 = slot_bias(a, seq_count // 2)
    bias4 = thirds(jnp.zeros((), F32), off_if((y == 1) | (y == 2)), jnp.zeros((), F32))[:, :256]

    def unit(level, c):
        if level == 0:
            bias = {0: thirds(no_prev, 0.0, 0.0), 3: thirds(0.0, 0.0, no_next)}.get(c)
            return (OFF[0] + BLOCK * c, BLOCK, kv0, BLOCK * c, 384, bias)
        if level == 1:
            return (OFF[1] + BLOCK * c, BLOCK, in1, BLOCK * (1 - c), 384, bias1[c])
        if level == 2:
            return (OFF[2], 128, in2, 0, 384, bias2)
        if level == 3:
            return (OFF[3], 64, in3, 0, 384, bias3)
        return (OFF[4], 32, in4, 0, 256, bias4)

    def forward(level, c=0):
        r0, n, ref, k0, m, bias = unit(level, c)
        rows, keys = pl.ds(r0, n), pl.ds(k0, m)
        sc = dot(qs[rows, :], ref[keys, :BLOCK], NT) * (scale * LOG2E)
        if bias is not None:
            sc = sc + bias
        top = jnp.max(sc, axis=1, keepdims=True)
        e = jnp.exp2(sc - top)
        pk[rows, :] = jnp.broadcast_to(top, (n, BLOCK))
        tot[rows, :] = jnp.broadcast_to(jnp.sum(e, axis=1, keepdims=True), (n, BLOCK))
        eb = e.astype(BF16)
        ee[rows, :m] = eb
        sm[rows, :] = dot(eb, ref[keys, BLOCK:])

    forward(0, 1)
    forward(0, 2)
    for level in (4, 3, 2):
        for slot in range(SLOT_COUNT[level]):
            forward_arrival(level, slot)
        forward(level)
    for slot in range(2):
        forward_arrival(1, slot)
    forward(1, 0)
    forward(1, 1)
    for slot in range(2):
        forward_arrival(0, slot)
    forward(0, 0)
    forward(0, 3)

    for b in range(4):
        where = [pl.ds(OFF[l] + (BLOCK >> l) * b, BLOCK >> l) for l in range(5)]
        peaks = [expand(pk[where[l], :], l) for l in range(5)]
        overall = functools.reduce(jnp.maximum, peaks)
        factors = [jnp.exp2(peaks[l] - overall) * float(1 << l) for l in range(5)]
        den = sum(factors[l] * expand(tot[where[l], :], l) for l in range(5))
        num = sum(factors[l] * expand(sm[where[l], :], l) for l in range(5))
        out = num / den
        att_ref[pl.ds(BLOCK * b, BLOCK), :] = dot(unperm, out.astype(BF16)).astype(BF16)
        cot = go[pl.ds(BLOCK * b, BLOCK), :]
        delta = jnp.broadcast_to(jnp.sum(cot * out, axis=1, keepdims=True), (BLOCK, BLOCK))
        cot, delta = cot / den, delta / den
        for l in range(5):
            gg[where[l], :] = group(factors[l] * cot, l)
            dd[where[l], :] = group(factors[l] * delta, l)

    def backward(level, c=0):
        r0, n, ref, k0, m, _ = unit(level, c)
        rows, keys = pl.ds(r0, n), pl.ds(k0, m)
        gb = gg[rows, :].astype(BF16)
        eb = ee[rows, :m]
        shift = jnp.concatenate([dd[rows, :]] * (m // BLOCK), axis=1)
        ds = eb.astype(F32) * (dot(gb, ref[keys, BLOCK:], NT) - shift)
        ds = (ds * scale).astype(BF16)
        dq[rows, :] = dot(ds, ref[keys, :BLOCK])
        return dot(ds, qs[rows, :], TN), dot(eb, gb, TN)

    def sides(parts):
        return ((parts[0], pl.ds(0, BLOCK)), (parts[1], pl.ds(BLOCK, BLOCK)))

    def start_back(level):
        for entry in peers:
            if entry[0] == level:
                back_copy(entry).start()

    for part, lanes in sides(backward(1, 0)):
        acc1[pl.ds(0, 384), lanes] = part
    for part, lanes in sides(backward(1, 1)):
        bk1[pl.ds(0, 128), lanes] = part[:128].astype(BF16)
        bk1[pl.ds(128, 256), lanes] = (part[128:] + acc1[pl.ds(0, 256), lanes]).astype(BF16)
        bk1[pl.ds(384, 128), lanes] = acc1[pl.ds(256, 128), lanes].astype(BF16)
    start_back(1)
    for level in (2, 3, 4):
        for part, lanes in sides(backward(level)):
            outbox[level][:, lanes] = part.astype(BF16)
        start_back(level)
    for part, lanes in sides(backward(0, 0)):
        bk0[pl.ds(0, 128), lanes] = part[:128].astype(BF16)
        acc0[pl.ds(0, 256), lanes] = part[128:]
    for part, lanes in sides(backward(0, 3)):
        acc0[pl.ds(256, 256), lanes] = part[:256]
        bk0[pl.ds(128, 128), lanes] = part[256:].astype(BF16)
    start_back(0)
    for part, lanes in sides(backward(0, 1)):
        acc0[pl.ds(0, 384), lanes] += part
    for part, lanes in sides(backward(0, 2)):
        acc0[pl.ds(128, 384), lanes] += part

    chunk = 4 * BLOCK // head_count

    def out_copy(index, src, dst, j):
        to = lax.rem(h + j, head_count)
        return pltpu.make_async_remote_copy(
            src_ref=src.at[pl.ds(pl.multiple_of(to * chunk, chunk), chunk), :],
            dst_ref=dst.at[:, pl.ds(pl.multiple_of(h * BLOCK, BLOCK), BLOCK)],
            send_sem=out_send.at[index, to],
            recv_sem=out_recv.at[index, h],
            device_id={"head": to},
            device_id_type=MESH,
        )

    def out_arrival(index, dst, j):
        frm = lax.rem(h + j, head_count)
        here = dst.at[:, pl.ds(pl.multiple_of(frm * BLOCK, BLOCK), BLOCK)]
        pltpu.make_async_remote_copy(
            src_ref=here, dst_ref=here,
            send_sem=out_send.at[index, frm], recv_sem=out_recv.at[index, frm],
            device_id={"head": h}, device_id_type=MESH,
        ).wait_recv()

    def keep(src, dst):
        dst[:, pl.ds(pl.multiple_of(h * BLOCK, BLOCK), BLOCK)] = src[
            pl.ds(pl.multiple_of(h * chunk, chunk), chunk), :
        ]

    for b in range(4):
        total = dq[pl.ds(OFF[4] + 8 * b, 8), :]
        for l in (3, 2, 1, 0):
            total = dq[pl.ds(OFF[l] + (BLOCK >> l) * b, BLOCK >> l), :] + 0.5 * expand(total, 1)
        oq[pl.ds(BLOCK * b, BLOCK), :] = dot(unperm, total.astype(BF16)).astype(BF16)
    for j in range(1, head_count):
        out_copy(0, oq, gq_ref, j).start()
    keep(oq, gq_ref)

    for level in (1, 2, 3, 4, 0):
        for slot in range(SLOT_COUNT[level]):
            back_arrival(level, slot)
    sum4 = sum(rx4[pl.ds(32 * i, 32), :].astype(F32) for i in range(8))
    sum3 = sum(rx3[pl.ds(64 * i, 64), :].astype(F32) for i in range(6)) + 0.5 * expand(sum4, 1)
    sum2 = sum(rx2[pl.ds(128 * i, 128), :].astype(F32) for i in range(3)) + 0.5 * expand(sum3, 1)
    for b in range(4):
        at = 64 * ((b + 2) % 4)
        sum1 = sum(rx1[pl.ds(256 * i + at, 64), :].astype(F32) for i in range(2))
        sum1 = sum1 + 0.5 * expand(sum2[32 * b : 32 * b + 32], 1)
        total = acc0[pl.ds(BLOCK * b, BLOCK), :] + 0.5 * expand(sum1, 1)
        if b == 0:
            total = total + rx0[pl.ds(0, BLOCK), :].astype(F32)
        if b == 3:
            total = total + rx0[pl.ds(BLOCK, BLOCK), :].astype(F32)
        done = dot(unperm, total.astype(BF16)).astype(BF16)
        ok[pl.ds(BLOCK * b, BLOCK), :] = done[:, :BLOCK]
        ov[pl.ds(BLOCK * b, BLOCK), :] = done[:, BLOCK:]
    for j in range(1, head_count):
        out_copy(1, ok, gk_ref, j).start()
        out_copy(2, ov, gv_ref, j).start()
    keep(ok, gk_ref)
    keep(ov, gv_ref)

    for entry in peers:
        forward_copy(entry).wait_send()
        back_copy(entry).wait_send()
    for index, src, dst in ((0, oq, gq_ref), (1, ok, gk_ref), (2, ov, gv_ref)):
        for j in range(1, head_count):
            out_copy(index, src, dst, j).wait_send()
            out_arrival(index, dst, j)


def solution(mesh):
    seq_count, head_count = mesh.shape["seq"], mesh.shape["head"]

    def step(queries, keys, values, grad_out):
        rows, width = queries.shape
        vmem = pl.BlockSpec(memory_space=pltpu.VMEM)
        grad = jax.ShapeDtypeStruct((rows // head_count, width * head_count), BF16)

        def wide(n, dtype=BF16):
            return pltpu.VMEM((n, WIDE), dtype)

        def stacked(dtype, width=BLOCK):
            return pltpu.VMEM((STACK, width), dtype)

        sems = pltpu.SemaphoreType.DMA
        return pl.pallas_call(
            functools.partial(kernel, seq_count, head_count),
            out_shape=(jax.ShapeDtypeStruct((rows, width), BF16), grad, grad, grad),
            in_specs=[vmem] * 4,
            out_specs=(vmem,) * 4,
            scratch_shapes=[
                wide(768), wide(256), wide(128), wide(64), wide(32),
                wide(512), wide(384), wide(384), wide(256),
                stacked(BF16), pltpu.VMEM((rows, width), F32), stacked(BF16, 384),
                stacked(F32), stacked(F32), stacked(F32), stacked(F32), stacked(F32), stacked(F32),
                wide(512, F32), wide(384, F32),
                wide(256), wide(512), wide(384), wide(384), wide(256),
                wide(256), wide(512), wide(384), wide(384), wide(256),
                pltpu.VMEM((rows, width), BF16), pltpu.VMEM((rows, width), BF16),
                pltpu.VMEM((rows, width), BF16),
                sems((SLOTS,)), sems((SLOTS,)), sems((SLOTS,)), sems((SLOTS,)),
                sems((3, head_count)), sems((3, head_count)),
            ],
            compiler_params=pltpu.CompilerParams(
                collective_id=0, has_side_effects=True, vmem_limit_bytes=48 * 1024 * 1024
            ),
        )(queries, keys, values, grad_out)

    return jax.shard_map(
        step,
        mesh=mesh,
        in_specs=(P("seq", "head"),) * 4,
        out_specs=(P("seq", "head"),) + (P(("seq", "head"), None),) * 3,
        check_vma=False,
    )
```

profile of v0, /device:TPU:1, one launch (start us, length us, event | category | flops | bytes accessed | tf_op | source)
XLA Modules:
  0.0 57.9 jit_solution(7961255408311508425)
XLA Ops:
  0.6 0.0 copy-start
  0.6 0.9 %copy-done = bf16[512,128]{1,0:T(8,128)(2,1)S(1)} copy-done((bf16[512,128]{1,0:T(8,128)(2,1)S(1)}, bf16[512,128]{1,0:T(8,128)(2,1)}, u32[]{:S(2)}) %copy-start) | copy-done | bytes 131096
  1.5 0.0 copy-start.1
  1.5 0.9 %copy-done.1 = bf16[512,128]{1,0:T(8,128)(2,1)S(1)} copy-done((bf16[512,128]{1,0:T(8,128)(2,1)S(1)}, bf16[512,128]{1,0:T(8,128)(2,1)}, u32[]{:S(2)}) %copy-start.1) | copy-done | bytes 131096
  2.4 0.0 copy-start.2
  2.4 0.9 %copy-done.2 = bf16[512,128]{1,0:T(8,128)(2,1)S(1)} copy-done((bf16[512,128]{1,0:T(8,128)(2,1)S(1)}, bf16[512,128]{1,0:T(8,128)(2,1)}, u32[]{:S(2)}) %copy-start.2) | copy-done | bytes 131096
  3.3 0.0 copy-start.3
  3.3 0.9 %copy-done.3 = bf16[512,128]{1,0:T(8,128)(2,1)S(1)} copy-done((bf16[512,128]{1,0:T(8,128)(2,1)S(1)}, bf16[512,128]{1,0:T(8,128)(2,1)}, u32[]{:S(2)}) %copy-start.3) | copy-done | bytes 131096
  4.3 51.0 %shard_map.75 = (bf16[512,128]{1,0:T(8,128)(2,1)S(1)}, bf16[32,2048]{1,0:T(8,128)(2,1)S(1)}, bf16[32,2048]{1,0:T(8,128)(2,1)S(1)}, bf16[32,2048]{1,0:T(8,128)(2,1)S(1)}) custom-call(bf16[512,128]{1,0:T(8,128)(2,1)S(1)} %copy-done, bf16[512,128]{1,0:T(8,128)(2,1)S(1)} %copy-done.1, bf16[512,128]{1,0:T(8,128)(2,1)S(1)} %copy-done.2, bf16[512,128]{1,0:T(8,128)(2,1)S(1)} %copy-done.3), custom_call_target="tpu_custom_call" | custom-call | tf_op jit(solution)/shard_map/pallas_call | solution.py:411
  55.3 0.7 %copy.12 = bf16[512,128]{1,0:T(8,128)(2,1)} copy(bf16[512,128]{1,0:T(8,128)(2,1)S(1)} %get-tuple-element.8) | data formatting | bytes 262144
  55.9 0.7 %copy.13 = bf16[32,2048]{1,0:T(8,128)(2,1)} copy(bf16[32,2048]{1,0:T(8,128)(2,1)S(1)} %get-tuple-element.9) | data formatting | bytes 262144
  56.6 0.7 %copy.14 = bf16[32,2048]{1,0:T(8,128)(2,1)} copy(bf16[32,2048]{1,0:T(8,128)(2,1)S(1)} %get-tuple-element.10) | data formatting | bytes 262144
  57.2 0.7 %copy.15 = bf16[32,2048]{1,0:T(8,128)(2,1)} copy(bf16[32,2048]{1,0:T(8,128)(2,1)S(1)} %get-tuple-element.11) | data formatting | bytes 262144
Async XLA Ops:
  0.6 0.9 %copy-start = (bf16[512,128]{1,0:T(8,128)(2,1)S(1)}, bf16[512,128]{1,0:T(8,128)(2,1)}, u32[]{:S(2)}) copy-start(bf16[512,128]{1,0:T(8,128)(2,1)} %q_ref.1) | copy-start | bytes 393220
  1.5 0.9 %copy-start.1 = (bf16[512,128]{1,0:T(8,128)(2,1)S(1)}, bf16[512,128]{1,0:T(8,128)(2,1)}, u32[]{:S(2)}) copy-start(bf16[512,128]{1,0:T(8,128)(2,1)} %k_ref.1) | copy-start | bytes 393220
  2.4 0.9 %copy-start.2 = (bf16[512,128]{1,0:T(8,128)(2,1)S(1)}, bf16[512,128]{1,0:T(8,128)(2,1)}, u32[]{:S(2)}) copy-start(bf16[512,128]{1,0:T(8,128)(2,1)} %v_ref.1) | copy-start | bytes 393220
  3.3 0.9 %copy-start.3 = (bf16[512,128]{1,0:T(8,128)(2,1)S(1)}, bf16[512,128]{1,0:T(8,128)(2,1)}, u32[]{:S(2)}) copy-start(bf16[512,128]{1,0:T(8,128)(2,1)} %g_ref.1) | copy-start | bytes 393220
where the time goes:
time: 58 us; the launch traced here: 57.9 us
  Pallas kernels  51 us (88%)
  local copies, waits for them, and re-layouts  6.23 us (11%)
  between operations  0.65 us (1%)
    pallas_call x1, Pallas kernels, step(): pl.pallas_call(functools.partial(kernel, seq_count, head_count), out_shap...  51 us
    unnamed x12, local copies, waits for them, and re-layouts  6.23 us

commit v1 on v0

--- a/solution.py
+++ b/solution.py
@@ -18,8 +18,7 @@
 STACK = 992
 SEM = (0, 2, 4, 7, 13)
 SLOTS = 21
-ROWS = (128, 256, 128, 64, 32)
-SLOT_COUNT = (2, 2, 3, 6, 8)
+ROWS = (128, 192, 128, 64, 32)
 
 NN = (((1,), (0,)), ((), ()))
 NT = (((1,), (1,)), ((), ()))
@@ -60,41 +59,58 @@
     y, x = lax.div(s, 4), lax.rem(s, 4)
 
     def third(i, n):
-        return lax.rem(i + n + 3 - 6 * lax.rem(i, 2), n)
+        turn = 3 - 6 * lax.rem(i, 2)
+        return lax.rem(i + n + turn, n), (i + turn >= 0) & (i + turn < n)
 
     blocks = seq_count // 2
     for f in range(4):
-        out.append((4, lax.rem(y + 2, 4) * 4 + f, f, x))
+        out.append((4, lax.rem(y + 2, 4) * 4 + f, f, x, None))
     for f in range(4):
-        out.append((4, (3 - y) * 4 + f, 4 + f, 4 + x))
-    far3 = third(a, blocks)
+        out.append((4, (3 - y) * 4 + f, 4 + f, 4 + x, (y == 0) | (y == 3)))
+    far3, far3_ok = third(a, blocks)
     for f in range(2):
-        out.append((3, far3 * 2 + f, 4 + f, 4 + e))
+        out.append((3, far3 * 2 + f, 4 + f, 4 + e, far3_ok))
     for f in range(2):
-        out.append((3, lax.rem(a + blocks - 2, blocks) * 2 + f, f, 2 + e))
-        out.append((3, lax.rem(a + 2, blocks) * 2 + f, 2 + f, e))
-    out.append((2, third(s, seq_count), 2, 2))
-    out.append((2, lax.rem(s + seq_count - 2, seq_count), 0, 1))
-    out.append((2, lax.rem(s + 2, seq_count), 1, 0))
-    out.append((1, prev, 0, 1))
-    out.append((1, after, 1, 0))
-    out.append((0, prev, 0, 1))
-    out.append((0, after, 1, 0))
+        out.append((3, lax.rem(a + blocks - 2, blocks) * 2 + f, f, 2 + e, a >= 2))
+        out.append((3, lax.rem(a + 2, blocks) * 2 + f, 2 + f, e, a + 2 < blocks))
+    far2, far2_ok = third(s, seq_count)
+    out.append((2, far2, 2, 2, far2_ok))
+    out.append((2, lax.rem(s + seq_count - 2, seq_count), 0, 1, s >= 2))
+    out.append((2, lax.rem(s + 2, seq_count), 1, 0, s + 2 < seq_count))
+    out.append((1, prev, 0, 1, s > 0))
+    out.append((1, after, 1, 0, s + 1 < seq_count))
+    out.append((0, prev, 0, 1, s > 0))
+    out.append((0, after, 1, 0, s + 1 < seq_count))
     return out
+
+
+def when(ok, act):
+    if ok is None:
+        act()
+    else:
+        pl.when(ok)(act)
 
 
 def kernel(
     seq_count, head_count,
-    q_ref, k_ref, v_ref, g_ref,
+    q_hbm, k_hbm, v_hbm, g_hbm,
     att_ref, gq_ref, gk_ref, gv_ref,
     kv0, kv1, kv2, kv3, kv4, in1, in2, in3, in4,
     qs, go, ee, pk, tot, sm, gg, dd, dq,
-    acc0, acc1, bk0, bk1, bk2, bk3, bk4, rx0, rx1, rx2, rx3, rx4,
-    oq, ok, ov,
+    acc0, acc1, edge, bk0, bk1, bk2, bk3, bk4, rx0, rx1, rx2, rx3, rx4,
+    oq, ok, ov, q_ref, k_ref, v_ref, g_ref, load_sem,
     send_sem, recv_sem, back_send, back_recv, out_send, out_recv,
 ):
     s, h = lax.axis_index("seq"), lax.axis_index("head")
     barrier = pltpu.get_barrier_semaphore()
+    loads = [
+        pltpu.make_async_copy(src, dst, load_sem.at[i])
+        for i, (src, dst) in enumerate(
+            ((k_hbm, k_ref), (v_hbm, v_ref), (q_hbm, q_ref), (g_hbm, g_ref))
+        )
+    ]
+    for load in loads:
+        load.start()
     for j in range(1, seq_count):
         pl.semaphore_signal(
             barrier, inc=1, device_id={"seq": lax.rem(s + j, seq_count)}, device_id_type=MESH
@@ -109,6 +125,8 @@
     perm = jnp.where(col == (row & 7) * 16 + (row >> 3), 1.0, 0.0).astype(BF16)
     unperm = jnp.where(col == (row & 15) * 8 + (row >> 4), 1.0, 0.0).astype(BF16)
 
+    loads[0].wait()
+    loads[1].wait()
     own = (kv0, kv1, kv2, kv3, kv4)
     tops = []
     for b in range(4):
@@ -116,7 +134,7 @@
         fine = dot(perm, jnp.concatenate([k_ref[rows, :], v_ref[rows, :]], axis=1))
         kv0[pl.ds(BLOCK + BLOCK * b, BLOCK), :] = fine.astype(BF16)
         m1 = halve(fine)
-        kv1[pl.ds(64 * ((b + 2) % 4), 64), :] = m1.astype(BF16)
+        kv1[pl.ds(64 * (3 - b), 64), :] = m1.astype(BF16)
         m2 = halve(m1)
         kv2[pl.ds(32 * b, 32), :] = m2.astype(BF16)
         m3 = halve(m2)
@@ -131,39 +149,53 @@
     outbox = (bk0, bk1, bk2, bk3, bk4)
     rxbox = (rx0, rx1, rx2, rx3, rx4)
 
-    def at_slot(ref, level, slot, spread=False):
+    def at_slot(ref, level, slot):
         n = ROWS[level]
-        if spread:
-            return ref.at[pl.ds(640 * slot, n), :]
         return ref.at[pl.ds(n * slot, n), :]
 
+    def in_slot(level, slot):
+        if level == 0:
+            return kv0.at[pl.ds(640 * slot, BLOCK), :]
+        if level == 1:
+            return in1.at[pl.ds(64 + 192 * slot, 192), :]
+        return at_slot(inbox[level], level, slot)
+
+    def out_slot(level, slot):
+        if level == 0:
+            return kv0.at[pl.ds(BLOCK + 384 * slot, BLOCK), :]
+        if level == 1:
+            return kv1.at[pl.ds(64 * slot, 192), :]
+        return own[level]
+
     def forward_copy(entry):
-        level, peer, slot, there = entry
-        if level == 0:
-            src = kv0.at[pl.ds(BLOCK + 384 * slot, BLOCK), :]
-        else:
-            src = own[level]
+        level, peer, slot, there, _ = entry
         return pltpu.make_async_remote_copy(
-            src_ref=src,
-            dst_ref=at_slot(inbox[level], level, there, level == 0),
+            src_ref=out_slot(level, slot),
+            dst_ref=in_slot(level, there),
             send_sem=send_sem.at[SEM[level] + slot],
             recv_sem=recv_sem.at[SEM[level] + there],
             device_id={"seq": peer},
             device_id_type=MESH,
         )
 
-    def forward_arrival(level, slot):
-        here = at_slot(inbox[level], level, slot, level == 0)
+    def forward_arrival(entry):
+        level, peer, slot = entry[:3]
+        here = in_slot(level, slot)
         pltpu.make_async_remote_copy(
             src_ref=here, dst_ref=here,
             send_sem=send_sem.at[SEM[level] + slot], recv_sem=recv_sem.at[SEM[level] + slot],
-            device_id={"seq": s}, device_id_type=MESH,
+            device_id={"seq": peer}, device_id_type=MESH,
         ).wait_recv()
 
+    def back_slot(level, slot):
+        if level == 1:
+            return bk1.at[pl.ds(64 + 192 * slot, 192), :]
+        return at_slot(outbox[level], level, slot)
+
     def back_copy(entry):
-        level, peer, slot, there = entry
+        level, peer, slot, there, _ = entry
         return pltpu.make_async_remote_copy(
-            src_ref=at_slot(outbox[level], level, slot),
+            src_ref=back_slot(level, slot),
             dst_ref=at_slot(rxbox[level], level, there),
             send_sem=back_send.at[SEM[level] + slot],
             recv_sem=back_recv.at[SEM[level] + there],
@@ -171,17 +203,32 @@
             device_id_type=MESH,
         )
 
-    def back_arrival(level, slot):
+    def back_arrival(entry):
+        level, peer, slot = entry[:3]
         here = at_slot(rxbox[level], level, slot)
         pltpu.make_async_remote_copy(
             src_ref=here, dst_ref=here,
             send_sem=back_send.at[SEM[level] + slot], recv_sem=back_recv.at[SEM[level] + slot],
-            device_id={"seq": s}, device_id_type=MESH,
+            device_id={"seq": peer}, device_id_type=MESH,
         ).wait_recv()
 
+    def at_level(level):
+        return [entry for entry in peers if entry[0] == level]
+
     for entry in peers:
-        forward_copy(entry).start()
-
+        when(entry[4], lambda: forward_copy(entry).start())
+
+    def clear(entry):
+        level, slot = entry[0], entry[2]
+        for ref in (in_slot(level, slot), at_slot(rxbox[level], level, slot)):
+            ref[...] = jnp.zeros(ref.shape, BF16)
+
+    for entry in peers:
+        if entry[4] is not None:
+            when(jnp.logical_not(entry[4]), lambda: clear(entry))
+
+    loads[2].wait()
+    loads[3].wait()
     tops = []
     for b in range(4):
         rows = pl.ds(BLOCK * b, BLOCK)
@@ -253,18 +300,20 @@
 
     forward(0, 1)
     forward(0, 2)
-    for level in (4, 3, 2):
-        for slot in range(SLOT_COUNT[level]):
-            forward_arrival(level, slot)
+    for entry in at_level(0):
+        when(entry[4], lambda: forward_arrival(entry))
+    in1[pl.ds(0, 64), :] = halve(kv0[pl.ds(0, BLOCK), :].astype(F32)).astype(BF16)
+    in1[pl.ds(448, 64), :] = halve(kv0[pl.ds(640, BLOCK), :].astype(F32)).astype(BF16)
+    forward(0, 0)
+    forward(0, 3)
+    for level in (3, 4, 2):
+        for entry in at_level(level):
+            when(entry[4], lambda: forward_arrival(entry))
         forward(level)
-    for slot in range(2):
-        forward_arrival(1, slot)
+    for entry in at_level(1):
+        when(entry[4], lambda: forward_arrival(entry))
     forward(1, 0)
     forward(1, 1)
-    for slot in range(2):
-        forward_arrival(0, slot)
-    forward(0, 0)
-    forward(0, 3)
 
     for b in range(4):
         where = [pl.ds(OFF[l] + (BLOCK >> l) * b, BLOCK >> l) for l in range(5)]
@@ -299,25 +348,29 @@
     def start_back(level):
         for entry in peers:
             if entry[0] == level:
-                back_copy(entry).start()
+                when(entry[4], lambda: back_copy(entry).start())
 
     for part, lanes in sides(backward(1, 0)):
         acc1[pl.ds(0, 384), lanes] = part
     for part, lanes in sides(backward(1, 1)):
-        bk1[pl.ds(0, 128), lanes] = part[:128].astype(BF16)
+        edge[pl.ds(0, 64), lanes] = part[:64]
+        bk1[pl.ds(64, 64), lanes] = part[64:128].astype(BF16)
         bk1[pl.ds(128, 256), lanes] = (part[128:] + acc1[pl.ds(0, 256), lanes]).astype(BF16)
-        bk1[pl.ds(384, 128), lanes] = acc1[pl.ds(256, 128), lanes].astype(BF16)
+        bk1[pl.ds(384, 64), lanes] = acc1[pl.ds(256, 64), lanes].astype(BF16)
+        edge[pl.ds(64, 64), lanes] = acc1[pl.ds(320, 64), lanes]
     start_back(1)
     for level in (2, 3, 4):
         for part, lanes in sides(backward(level)):
             outbox[level][:, lanes] = part.astype(BF16)
         start_back(level)
     for part, lanes in sides(backward(0, 0)):
-        bk0[pl.ds(0, 128), lanes] = part[:128].astype(BF16)
+        fold = 0.5 * expand(edge[pl.ds(0, 64), lanes], 1)
+        bk0[pl.ds(0, 128), lanes] = (part[:128] + fold).astype(BF16)
         acc0[pl.ds(0, 256), lanes] = part[128:]
     for part, lanes in sides(backward(0, 3)):
         acc0[pl.ds(256, 256), lanes] = part[:256]
-        bk0[pl.ds(128, 128), lanes] = part[256:].astype(BF16)
+        fold = 0.5 * expand(edge[pl.ds(64, 64), lanes], 1)
+        bk0[pl.ds(128, 128), lanes] = (part[256:] + fold).astype(BF16)
     start_back(0)
     for part, lanes in sides(backward(0, 1)):
         acc0[pl.ds(0, 384), lanes] += part
@@ -361,14 +414,17 @@
     keep(oq, gq_ref)
 
     for level in (1, 2, 3, 4, 0):
-        for slot in range(SLOT_COUNT[level]):
-            back_arrival(level, slot)
+        for entry in at_level(level):
+            when(entry[4], lambda: back_arrival(entry))
     sum4 = sum(rx4[pl.ds(32 * i, 32), :].astype(F32) for i in range(8))
     sum3 = sum(rx3[pl.ds(64 * i, 64), :].astype(F32) for i in range(6)) + 0.5 * expand(sum4, 1)
     sum2 = sum(rx2[pl.ds(128 * i, 128), :].astype(F32) for i in range(3)) + 0.5 * expand(sum3, 1)
     for b in range(4):
-        at = 64 * ((b + 2) % 4)
-        sum1 = sum(rx1[pl.ds(256 * i + at, 64), :].astype(F32) for i in range(2))
+        sum1 = jnp.zeros((64, WIDE), F32)
+        if b > 0:
+            sum1 = sum1 + rx1[pl.ds(64 * (3 - b), 64), :].astype(F32)
+        if b < 3:
+            sum1 = sum1 + rx1[pl.ds(192 + 64 * (2 - b), 64), :].astype(F32)
         sum1 = sum1 + 0.5 * expand(sum2[32 * b : 32 * b + 32], 1)
         total = acc0[pl.ds(BLOCK * b, BLOCK), :] + 0.5 * expand(sum1, 1)
         if b == 0:
@@ -385,14 +441,24 @@
     keep(ov, gv_ref)
 
     for entry in peers:
-        forward_copy(entry).wait_send()
-        back_copy(entry).wait_send()
+        when(entry[4], lambda: (forward_copy(entry).wait_send(), back_copy(entry).wait_send()) and None)
     for index, src, dst in ((0, oq, gq_ref), (1, ok, gk_ref), (2, ov, gv_ref)):
         for j in range(1, head_count):
             out_copy(index, src, dst, j).wait_send()
             out_arrival(index, dst, j)
 
 
+def write_out(a, b, c, d, a_out, b_out, c_out, d_out, sem):
+    copies = [
+        pltpu.make_async_copy(src, dst, sem.at[i])
+        for i, (src, dst) in enumerate(((a, a_out), (b, b_out), (c, c_out), (d, d_out)))
+    ]
+    for copy in copies:
+        copy.start()
+    for copy in copies:
+        copy.wait()
+
+
 def solution(mesh):
     seq_count, head_count = mesh.shape["seq"], mesh.shape["head"]
 
@@ -408,28 +474,36 @@
             return pltpu.VMEM((STACK, width), dtype)
 
         sems = pltpu.SemaphoreType.DMA
-        return pl.pallas_call(
+        results = pl.pallas_call(
             functools.partial(kernel, seq_count, head_count),
             out_shape=(jax.ShapeDtypeStruct((rows, width), BF16), grad, grad, grad),
-            in_specs=[vmem] * 4,
+            in_specs=[pl.BlockSpec(memory_space=pltpu.HBM)] * 4,
             out_specs=(vmem,) * 4,
             scratch_shapes=[
                 wide(768), wide(256), wide(128), wide(64), wide(32),
                 wide(512), wide(384), wide(384), wide(256),
                 stacked(BF16), pltpu.VMEM((rows, width), F32), stacked(BF16, 384),
                 stacked(F32), stacked(F32), stacked(F32), stacked(F32), stacked(F32), stacked(F32),
-                wide(512, F32), wide(384, F32),
+                wide(512, F32), wide(384, F32), wide(128, F32),
                 wide(256), wide(512), wide(384), wide(384), wide(256),
-                wide(256), wide(512), wide(384), wide(384), wide(256),
-                pltpu.VMEM((rows, width), BF16), pltpu.VMEM((rows, width), BF16),
-                pltpu.VMEM((rows, width), BF16),
+                wide(256), wide(384), wide(384), wide(384), wide(256),
+                *[pltpu.VMEM((rows, width), BF16) for _ in range(7)],
+                sems((4,)),
                 sems((SLOTS,)), sems((SLOTS,)), sems((SLOTS,)), sems((SLOTS,)),
                 sems((3, head_count)), sems((3, head_count)),
             ],
             compiler_params=pltpu.CompilerParams(
-                collective_id=0, has_side_effects=True, vmem_limit_bytes=48 * 1024 * 1024
+                collective_id=0, has_side_effects=True, vmem_limit_bytes=56000000
             ),
         )(queries, keys, values, grad_out)
+        return pl.pallas_call(
+            write_out,
+            out_shape=tuple(jax.ShapeDtypeStruct(r.shape, r.dtype) for r in results),
+            in_specs=[vmem] * 4,
+            out_specs=(pl.BlockSpec(memory_space=pltpu.HBM),) * 4,
+            scratch_shapes=[sems((4,))],
+            compiler_params=pltpu.CompilerParams(vmem_limit_bytes=1024 * 1024),
+        )(*results)
 
     return jax.shard_map(
         step,

time: 58 us -> 48.5 us (0.84)
  local copies, waits for them, and re-layouts: 6.23 us -> 0 us
  Pallas kernels: 51 us -> 47.7 us
    unnamed x12 -> x0, local copies, waits for them, and re-layouts: 6.23 us -> none
    pallas_call x1, Pallas kernels: 51 us -> 46.9 us  [step(): pl.pallas_call(functools.partial(kernel, seq_count, head_count), out_shap...]
    pallas_call x0 -> x1, Pallas kernels: none -> 0.82 us  [step(): pl.pallas_call(write_out, out_shape=tuple((jax.ShapeDtypeStruct(r.shape,...]
where the time goes in v1:
time: 48.5 us; the launch traced here: 48.4 us
  Pallas kernels  47.7 us (98%)
  between operations  0.64 us (1%)
    pallas_call x1, Pallas kernels, step(): pl.pallas_call(functools.partial(kernel, seq_count, head_count), out_shap...  46.9 us

profile of v1, /device:TPU:1, one launch (start us, length us, event | category | flops | bytes accessed | tf_op | source)
XLA Modules:
  0.0 48.4 jit_solution(10581488349235133051)
XLA Ops:
  0.6 46.9 %shard_map.75 = (bf16[512,128]{1,0:T(8,128)(2,1)S(1)}, bf16[32,2048]{1,0:T(8,128)(2,1)S(1)}, bf16[32,2048]{1,0:T(8,128)(2,1)S(1)}, bf16[32,2048]{1,0:T(8,128)(2,1)S(1)}) custom-call(bf16[512,128]{1,0:T(8,128)(2,1)} %q_hbm.1, bf16[512,128]{1,0:T(8,128)(2,1)} %k_hbm.1, bf16[512,128]{1,0:T(8,128)(2,1)} %v_hbm.1, bf16[512,128]{1,0:T(8,128)(2,1)} %g_hbm.1), custom_call_target="tpu_custom_call" | custom-call | tf_op jit(solution)/shard_map/pallas_call | solution.py:477
  47.6 0.8 %shard_map.76 = (bf16[512,128]{1,0:T(8,128)(2,1)}, bf16[32,2048]{1,0:T(8,128)(2,1)}, bf16[32,2048]{1,0:T(8,128)(2,1)}, bf16[32,2048]{1,0:T(8,128)(2,1)}) custom-call(bf16[512,128]{1,0:T(8,128)(2,1)S(1)} %get-tuple-element.8.a, bf16[32,2048]{1,0:T(8,128)(2,1)S(1)} %get-tuple-element.9.b, bf16[32,2048]{1,0:T(8,128)(2,1)S(1)} %get-tuple-element.10.c, ...), custom_call_target="tpu_custom_call" | custom-call | tf_op jit(solution)/shard_map/pallas_call | solution.py:499

commit v2 on v1

--- a/solution.py
+++ b/solution.py
@@ -20,6 +20,8 @@
 SLOTS = 21
 ROWS = (128, 192, 128, 64, 32)
 
+SEND_ORDER = (0, 1, 4, 3, 2)
+BACK_ORDER = (2, 3, 4)
 NN = (((1,), (0,)), ((), ()))
 NT = (((1,), (1,)), ((), ()))
 TN = (((0,), (0,)), ((), ()))
@@ -98,7 +100,7 @@
     kv0, kv1, kv2, kv3, kv4, in1, in2, in3, in4,
     qs, go, ee, pk, tot, sm, gg, dd, dq,
     acc0, acc1, edge, bk0, bk1, bk2, bk3, bk4, rx0, rx1, rx2, rx3, rx4,
-    oq, ok, ov, q_ref, k_ref, v_ref, g_ref, load_sem,
+    oq, ok, ov, oc, coarse, q_ref, k_ref, v_ref, g_ref, load_sem,
     send_sem, recv_sem, back_send, back_recv, out_send, out_recv,
 ):
     s, h = lax.axis_index("seq"), lax.axis_index("head")
@@ -215,8 +217,9 @@
     def at_level(level):
         return [entry for entry in peers if entry[0] == level]
 
-    for entry in peers:
-        when(entry[4], lambda: forward_copy(entry).start())
+    for level in SEND_ORDER:
+        for entry in at_level(level):
+            when(entry[4], lambda: forward_copy(entry).start())
 
     def clear(entry):
         level, slot = entry[0], entry[2]
@@ -300,20 +303,19 @@
 
     forward(0, 1)
     forward(0, 2)
-    for entry in at_level(0):
-        when(entry[4], lambda: forward_arrival(entry))
-    in1[pl.ds(0, 64), :] = halve(kv0[pl.ds(0, BLOCK), :].astype(F32)).astype(BF16)
-    in1[pl.ds(448, 64), :] = halve(kv0[pl.ds(640, BLOCK), :].astype(F32)).astype(BF16)
-    forward(0, 0)
-    forward(0, 3)
-    for level in (3, 4, 2):
+    for level in SEND_ORDER:
         for entry in at_level(level):
             when(entry[4], lambda: forward_arrival(entry))
-        forward(level)
-    for entry in at_level(1):
-        when(entry[4], lambda: forward_arrival(entry))
-    forward(1, 0)
-    forward(1, 1)
+        if level == 0:
+            in1[pl.ds(0, 64), :] = halve(kv0[pl.ds(0, BLOCK), :].astype(F32)).astype(BF16)
+            in1[pl.ds(448, 64), :] = halve(kv0[pl.ds(640, BLOCK), :].astype(F32)).astype(BF16)
+            forward(0, 0)
+            forward(0, 3)
+        elif level == 1:
+            forward(1, 0)
+            forward(1, 1)
+        else:
+            forward(level)
 
     for b in range(4):
         where = [pl.ds(OFF[l] + (BLOCK >> l) * b, BLOCK >> l) for l in range(5)]
@@ -322,11 +324,12 @@
         factors = [jnp.exp2(peaks[l] - overall) * float(1 << l) for l in range(5)]
         den = sum(factors[l] * expand(tot[where[l], :], l) for l in range(5))
         num = sum(factors[l] * expand(sm[where[l], :], l) for l in range(5))
-        out = num / den
+        inverse = 1.0 / den
+        out = num * inverse
         att_ref[pl.ds(BLOCK * b, BLOCK), :] = dot(unperm, out.astype(BF16)).astype(BF16)
         cot = go[pl.ds(BLOCK * b, BLOCK), :]
         delta = jnp.broadcast_to(jnp.sum(cot * out, axis=1, keepdims=True), (BLOCK, BLOCK))
-        cot, delta = cot / den, delta / den
+        cot, delta = cot * inverse, delta * inverse
         for l in range(5):
             gg[where[l], :] = group(factors[l] * cot, l)
             dd[where[l], :] = group(factors[l] * delta, l)
@@ -359,10 +362,6 @@
         bk1[pl.ds(384, 64), lanes] = acc1[pl.ds(256, 64), lanes].astype(BF16)
         edge[pl.ds(64, 64), lanes] = acc1[pl.ds(320, 64), lanes]
     start_back(1)
-    for level in (2, 3, 4):
-        for part, lanes in sides(backward(level)):
-            outbox[level][:, lanes] = part.astype(BF16)
-        start_back(level)
     for part, lanes in sides(backward(0, 0)):
         fold = 0.5 * expand(edge[pl.ds(0, 64), lanes], 1)
         bk0[pl.ds(0, 128), lanes] = (part[:128] + fold).astype(BF16)
@@ -372,6 +371,10 @@
         fold = 0.5 * expand(edge[pl.ds(64, 64), lanes], 1)
         bk0[pl.ds(128, 128), lanes] = (part[256:] + fold).astype(BF16)
     start_back(0)
+    for level in BACK_ORDER:
+        for part, lanes in sides(backward(level)):
+            outbox[level][:, lanes] = part.astype(BF16)
+        start_back(level)
     for part, lanes in sides(backward(0, 1)):
         acc0[pl.ds(0, 384), lanes] += part
     for part, lanes in sides(backward(0, 2)):
@@ -381,8 +384,9 @@
 
     def out_copy(index, src, dst, j):
         to = lax.rem(h + j, head_count)
+        n = dst.shape[0]
         return pltpu.make_async_remote_copy(
-            src_ref=src.at[pl.ds(pl.multiple_of(to * chunk, chunk), chunk), :],
+            src_ref=src.at[pl.ds(pl.multiple_of(to * n, n), n), :],
             dst_ref=dst.at[:, pl.ds(pl.multiple_of(h * BLOCK, BLOCK), BLOCK)],
             send_sem=out_send.at[index, to],
             recv_sem=out_recv.at[index, h],
@@ -401,7 +405,7 @@
 
     def keep(src, dst):
         dst[:, pl.ds(pl.multiple_of(h * BLOCK, BLOCK), BLOCK)] = src[
-            pl.ds(pl.multiple_of(h * chunk, chunk), chunk), :
+            pl.ds(pl.multiple_of(h * dst.shape[0], dst.shape[0]), dst.shape[0]), :
         ]
 
     for b in range(4):
@@ -413,19 +417,14 @@
         out_copy(0, oq, gq_ref, j).start()
     keep(oq, gq_ref)
 
-    for level in (1, 2, 3, 4, 0):
-        for entry in at_level(level):
-            when(entry[4], lambda: back_arrival(entry))
-    sum4 = sum(rx4[pl.ds(32 * i, 32), :].astype(F32) for i in range(8))
-    sum3 = sum(rx3[pl.ds(64 * i, 64), :].astype(F32) for i in range(6)) + 0.5 * expand(sum4, 1)
-    sum2 = sum(rx2[pl.ds(128 * i, 128), :].astype(F32) for i in range(3)) + 0.5 * expand(sum3, 1)
+    for entry in at_level(1) + at_level(0):
+        when(entry[4], lambda: back_arrival(entry))
     for b in range(4):
         sum1 = jnp.zeros((64, WIDE), F32)
         if b > 0:
             sum1 = sum1 + rx1[pl.ds(64 * (3 - b), 64), :].astype(F32)
         if b < 3:
             sum1 = sum1 + rx1[pl.ds(192 + 64 * (2 - b), 64), :].astype(F32)
-        sum1 = sum1 + 0.5 * expand(sum2[32 * b : 32 * b + 32], 1)
         total = acc0[pl.ds(BLOCK * b, BLOCK), :] + 0.5 * expand(sum1, 1)
         if b == 0:
             total = total + rx0[pl.ds(0, BLOCK), :].astype(F32)
@@ -440,12 +439,34 @@
     keep(ok, gk_ref)
     keep(ov, gv_ref)
 
+    for entry in at_level(2) + at_level(3) + at_level(4):
+        when(entry[4], lambda: back_arrival(entry))
+    sum4 = sum(rx4[pl.ds(32 * i, 32), :].astype(F32) for i in range(8))
+    sum3 = sum(rx3[pl.ds(64 * i, 64), :].astype(F32) for i in range(6)) + 0.5 * expand(sum4, 1)
+    sum2 = sum(rx2[pl.ds(128 * i, 128), :].astype(F32) for i in range(3)) + 0.5 * expand(sum3, 1)
+    r64, c64 = row[:64, :64], col[:64, :64]
+    nth = 8 * (r64 >> 4) + (r64 & 7)
+    pick = jnp.where(
+        c64 == 32 * ((r64 >> 3) & 1) + 8 * (nth & 3) + (nth >> 2), 1.0, 0.0
+    ).astype(BF16)
+    for b in range(4):
+        part = sum2[32 * b : 32 * b + 32]
+        part = jnp.concatenate([part[:, :BLOCK], part[:, BLOCK:]], axis=0).astype(BF16)
+        oc[pl.ds(64 * b, 64), :] = dot(pick, part).astype(BF16)
+    for j in range(1, head_count):
+        out_copy(3, oc, coarse, j).start()
+    keep(oc, coarse)
     for entry in peers:
         when(entry[4], lambda: (forward_copy(entry).wait_send(), back_copy(entry).wait_send()) and None)
-    for index, src, dst in ((0, oq, gq_ref), (1, ok, gk_ref), (2, ov, gv_ref)):
+    for index, src, dst in ((0, oq, gq_ref), (1, ok, gk_ref), (2, ov, gv_ref), (3, oc, coarse)):
         for j in range(1, head_count):
             out_copy(index, src, dst, j).wait_send()
             out_arrival(index, dst, j)
+    r16, c16 = row[:64, :16], col[:64, :16]
+    spread = jnp.where(c16 == 8 * (r16 >> 5) + ((r16 & 31) >> 2), 0.25, 0.0).astype(BF16)
+    more = dot(spread, coarse[...])
+    gk_ref[...] = (gk_ref[...].astype(F32) + more[:chunk]).astype(BF16)
+    gv_ref[...] = (gv_ref[...].astype(F32) + more[chunk:]).astype(BF16)
 
 
 def write_out(a, b, c, d, a_out, b_out, c_out, d_out, sem):
@@ -487,10 +508,12 @@
                 wide(512, F32), wide(384, F32), wide(128, F32),
                 wide(256), wide(512), wide(384), wide(384), wide(256),
                 wide(256), wide(384), wide(384), wide(384), wide(256),
-                *[pltpu.VMEM((rows, width), BF16) for _ in range(7)],
+                *[pltpu.VMEM((rows, width), BF16) for _ in range(3)],
+                pltpu.VMEM((256, BLOCK), BF16), pltpu.VMEM((16, width * head_count), BF16),
+                *[pltpu.VMEM((rows, width), BF16) for _ in range(4)],
                 sems((4,)),
                 sems((SLOTS,)), sems((SLOTS,)), sems((SLOTS,)), sems((SLOTS,)),
-                sems((3, head_count)), sems((3, head_count)),
+                sems((4, head_count)), sems((4, head_count)),
             ],
             compiler_params=pltpu.CompilerParams(
                 collective_id=0, has_side_effects=True, vmem_limit_bytes=56000000

time: 48.5 us -> 44.8 us (0.924)
  Pallas kernels: 47.7 us -> 44 us
    pallas_call x1, Pallas kernels: 46.9 us -> 43.2 us  [step(): pl.pallas_call(functools.partial(kernel, seq_count, head_count), out_shap...]
where the time goes in v2:
time: 44.8 us; the launch traced here: 44.7 us
  Pallas kernels  44 us (98%)
  between operations  0.64 us (1%)
    pallas_call x1, Pallas kernels, step(): pl.pallas_call(functools.partial(kernel, seq_count, head_count), out_shap...  43.2 us

profile of v2, /device:TPU:1, one launch (start us, length us, event | category | flops | bytes accessed | tf_op | source)
XLA Modules:
  0.0 44.7 jit_solution(6524319123495460376)
XLA Ops:
  0.6 43.2 %shard_map.75 = (bf16[512,128]{1,0:T(8,128)(2,1)S(1)}, bf16[32,2048]{1,0:T(8,128)(2,1)S(1)}, bf16[32,2048]{1,0:T(8,128)(2,1)S(1)}, bf16[32,2048]{1,0:T(8,128)(2,1)S(1)}) custom-call(bf16[512,128]{1,0:T(8,128)(2,1)} %q_hbm.1, bf16[512,128]{1,0:T(8,128)(2,1)} %k_hbm.1, bf16[512,128]{1,0:T(8,128)(2,1)} %v_hbm.1, bf16[512,128]{1,0:T(8,128)(2,1)} %g_hbm.1), custom_call_target="tpu_custom_call" | custom-call | tf_op jit(solution)/shard_map/pallas_call | solution.py:498
  43.9 0.8 %shard_map.76 = (bf16[512,128]{1,0:T(8,128)(2,1)}, bf16[32,2048]{1,0:T(8,128)(2,1)}, bf16[32,2048]{1,0:T(8,128)(2,1)}, bf16[32,2048]{1,0:T(8,128)(2,1)}) custom-call(bf16[512,128]{1,0:T(8,128)(2,1)S(1)} %get-tuple-element.8.a, bf16[32,2048]{1,0:T(8,128)(2,1)S(1)} %get-tuple-element.9.b, bf16[32,2048]{1,0:T(8,128)(2,1)S(1)} %get-tuple-element.10.c, ...), custom_call_target="tpu_custom_call" | custom-call | tf_op jit(solution)/shard_map/pallas_call | solution.py:522

commit v3 on v2

--- a/solution.py
+++ b/solution.py
@@ -14,14 +14,18 @@
 BF16 = jnp.bfloat16
 LOG2E = 1.4426950408889634
 MESH = pl.DeviceIdType.MESH
+OUT_SEM = (0, 2, 4, 7, 13)
+OUT_SLOTS = 21
+OUT_ROWS = (128, 192, 128, 64, 32)
 OFF = (0, 512, 768, 896, 960)
 STACK = 992
-SEM = (0, 2, 4, 7, 13)
-SLOTS = 21
-ROWS = (128, 192, 128, 64, 32)
+SEM = (0, 2, 4, 7, 10)
+ROW_SEM = 12
+SLOTS = 16
+ROWS = (128, 192, 128, 128, 128)
 
 SEND_ORDER = (0, 1, 4, 3, 2)
-BACK_ORDER = (2, 3, 4)
+FAR_FIRST = (8, 7, 9, 6, 10, 5, 11, 4, 12, 3, 13, 2, 14, 1, 15)
 NN = (((1,), (0,)), ((), ()))
 NT = (((1,), (1,)), ((), ()))
 TN = (((0,), (0,)), ((), ()))
@@ -56,33 +60,55 @@
 
 def peers_of(s, seq_count):
     out = []
+
+    def both(level, peer, slot, there, ok):
+        out.append((level, peer, slot, there, ok, peer, ok))
+
+    y, x = lax.div(s, 4), lax.rem(s, 4)
+    up, down = lax.rem(s + seq_count - 4, seq_count), lax.rem(s + 4, seq_count)
+    up_ok, down_ok = y > 0, y < 3
+    right = x >= 2
+    both(4, lax.rem(s + 8, seq_count), 0, 0, None)
+    both(4, (3 - y) * 4 + x, 1, 1, (y == 0) | (y == 3))
+    both(3, up, 0, 1, up_ok)
+    both(3, down, 1, 0, down_ok)
+    out.append((
+        3, jnp.where(right, down, up), 2, 2,
+        (right & down_ok) | (jnp.logical_not(right) & up_ok),
+        jnp.where(right, up, down), (right & up_ok) | (jnp.logical_not(right) & down_ok),
+    ))
+    turn = 3 - 6 * lax.rem(s, 2)
+    far = lax.rem(s + seq_count + turn, seq_count)
+    both(2, far, 2, 2, (s + turn >= 0) & (s + turn < seq_count))
+    both(2, lax.rem(s + seq_count - 2, seq_count), 0, 1, s >= 2)
+    both(2, lax.rem(s + 2, seq_count), 1, 0, s + 2 < seq_count)
     prev, after = lax.rem(s + seq_count - 1, seq_count), lax.rem(s + 1, seq_count)
+    for level in (1, 0):
+        both(level, prev, 0, 1, s > 0)
+        both(level, after, 1, 0, s + 1 < seq_count)
+    return out
+
+
+def direct_of(s, seq_count):
+    out = []
+
+    def both(level, peer, slot, there, ok):
+        out.append((level, peer, slot, there, ok, peer, ok))
+
     a, e = lax.div(s, 2), lax.rem(s, 2)
     y, x = lax.div(s, 4), lax.rem(s, 4)
-
-    def third(i, n):
-        turn = 3 - 6 * lax.rem(i, 2)
-        return lax.rem(i + n + turn, n), (i + turn >= 0) & (i + turn < n)
-
     blocks = seq_count // 2
     for f in range(4):
-        out.append((4, lax.rem(y + 2, 4) * 4 + f, f, x, None))
+        both(4, lax.rem(y + 2, 4) * 4 + f, f, x, None)
     for f in range(4):
-        out.append((4, (3 - y) * 4 + f, 4 + f, 4 + x, (y == 0) | (y == 3)))
-    far3, far3_ok = third(a, blocks)
+        both(4, (3 - y) * 4 + f, 4 + f, 4 + x, (y == 0) | (y == 3))
+    turn = 3 - 6 * lax.rem(a, 2)
+    far = lax.rem(a + blocks + turn, blocks)
     for f in range(2):
-        out.append((3, far3 * 2 + f, 4 + f, 4 + e, far3_ok))
+        both(3, far * 2 + f, 4 + f, 4 + e, (a + turn >= 0) & (a + turn < blocks))
     for f in range(2):
-        out.append((3, lax.rem(a + blocks - 2, blocks) * 2 + f, f, 2 + e, a >= 2))
-        out.append((3, lax.rem(a + 2, blocks) * 2 + f, 2 + f, e, a + 2 < blocks))
-    far2, far2_ok = third(s, seq_count)
-    out.append((2, far2, 2, 2, far2_ok))
-    out.append((2, lax.rem(s + seq_count - 2, seq_count), 0, 1, s >= 2))
-    out.append((2, lax.rem(s + 2, seq_count), 1, 0, s + 2 < seq_count))
-    out.append((1, prev, 0, 1, s > 0))
-    out.append((1, after, 1, 0, s + 1 < seq_count))
-    out.append((0, prev, 0, 1, s > 0))
-    out.append((0, after, 1, 0, s + 1 < seq_count))
+        both(3, lax.rem(a + blocks - 2, blocks) * 2 + f, f, 2 + e, a >= 2)
+        both(3, lax.rem(a + 2, blocks) * 2 + f, 2 + f, e, a + 2 < blocks)
     return out
 
 
@@ -100,7 +126,7 @@
     kv0, kv1, kv2, kv3, kv4, in1, in2, in3, in4,
     qs, go, ee, pk, tot, sm, gg, dd, dq,
     acc0, acc1, edge, bk0, bk1, bk2, bk3, bk4, rx0, rx1, rx2, rx3, rx4,
-    oq, ok, ov, oc, coarse, q_ref, k_ref, v_ref, g_ref, load_sem,
+    panel, cots, parts, oq, ok, ov, oc, coarse, q_ref, k_ref, v_ref, g_ref, load_sem,
     send_sem, recv_sem, back_send, back_recv, out_send, out_recv,
 ):
     s, h = lax.axis_index("seq"), lax.axis_index("head")
@@ -113,6 +139,7 @@
     ]
     for load in loads:
         load.start()
+    y, x = lax.div(s, 4), lax.rem(s, 4)
     for j in range(1, seq_count):
         pl.semaphore_signal(
             barrier, inc=1, device_id={"seq": lax.rem(s + j, seq_count)}, device_id_type=MESH
@@ -129,7 +156,6 @@
 
     loads[0].wait()
     loads[1].wait()
-    own = (kv0, kv1, kv2, kv3, kv4)
     tops = []
     for b in range(4):
         rows = pl.ds(BLOCK * b, BLOCK)
@@ -147,9 +173,12 @@
     pl.semaphore_wait(barrier, seq_count - 1 + head_count - 1)
 
     peers = peers_of(s, seq_count)
+    outward = [entry for entry in peers if entry[0] < 3] + direct_of(s, seq_count)
     inbox = (kv0, in1, in2, in3, in4)
     outbox = (bk0, bk1, bk2, bk3, bk4)
     rxbox = (rx0, rx1, rx2, rx3, rx4)
+
+    right = lax.div(x, 2)
 
     def at_slot(ref, level, slot):
         n = ROWS[level]
@@ -160,22 +189,23 @@
             return kv0.at[pl.ds(640 * slot, BLOCK), :]
         if level == 1:
             return in1.at[pl.ds(64 + 192 * slot, 192), :]
-        return at_slot(inbox[level], level, slot)
+        n = OUT_ROWS[level]
+        return inbox[level].at[pl.ds(n * slot, n), :]
 
     def out_slot(level, slot):
         if level == 0:
             return kv0.at[pl.ds(BLOCK + 384 * slot, BLOCK), :]
         if level == 1:
             return kv1.at[pl.ds(64 * slot, 192), :]
-        return own[level]
+        return (kv2, kv3, kv4)[level - 2]
 
     def forward_copy(entry):
-        level, peer, slot, there, _ = entry
+        level, peer, slot, there = entry[:4]
         return pltpu.make_async_remote_copy(
             src_ref=out_slot(level, slot),
             dst_ref=in_slot(level, there),
-            send_sem=send_sem.at[SEM[level] + slot],
-            recv_sem=recv_sem.at[SEM[level] + there],
+            send_sem=send_sem.at[OUT_SEM[level] + slot],
+            recv_sem=recv_sem.at[OUT_SEM[level] + there],
             device_id={"seq": peer},
             device_id_type=MESH,
         )
@@ -185,7 +215,7 @@
         here = in_slot(level, slot)
         pltpu.make_async_remote_copy(
             src_ref=here, dst_ref=here,
-            send_sem=send_sem.at[SEM[level] + slot], recv_sem=recv_sem.at[SEM[level] + slot],
+            send_sem=send_sem.at[OUT_SEM[level] + slot], recv_sem=recv_sem.at[OUT_SEM[level] + slot],
             device_id={"seq": peer}, device_id_type=MESH,
         ).wait_recv()
 
@@ -195,7 +225,7 @@
         return at_slot(outbox[level], level, slot)
 
     def back_copy(entry):
-        level, peer, slot, there, _ = entry
+        level, _, slot, there, _, peer, _ = entry
         return pltpu.make_async_remote_copy(
             src_ref=back_slot(level, slot),
             dst_ref=at_slot(rxbox[level], level, there),
@@ -217,18 +247,51 @@
     def at_level(level):
         return [entry for entry in peers if entry[0] == level]
 
+    def row_copy(src, dst, sends, recvs, d):
+        to = lax.rem(x + d, 4)
+        return pltpu.make_async_remote_copy(
+            src_ref=src(to),
+            dst_ref=dst.at[pl.ds(pl.multiple_of(x * 64, 64), 64), :],
+            send_sem=sends.at[ROW_SEM + to],
+            recv_sem=recvs.at[ROW_SEM + x],
+            device_id={"seq": y * 4 + to},
+            device_id_type=MESH,
+        )
+
+    def row_arrival(dst, sends, recvs, d):
+        frm = lax.rem(x + d, 4)
+        here = dst.at[pl.ds(pl.multiple_of(frm * 64, 64), 64), :]
+        pltpu.make_async_remote_copy(
+            src_ref=here, dst_ref=here,
+            send_sem=sends.at[ROW_SEM + frm], recv_sem=recvs.at[ROW_SEM + frm],
+            device_id={"seq": y * 4 + frm}, device_id_type=MESH,
+        ).wait_recv()
+
+    def piece_back(d):
+        return row_copy(
+            lambda to: cots.at[pl.ds(pl.multiple_of(to * 64, 64), 64), :],
+            parts, back_send, back_recv, d,
+        )
+
+    def out_level(level):
+        return [entry for entry in outward if entry[0] == level]
+
     for level in SEND_ORDER:
-        for entry in at_level(level):
+        for entry in out_level(level):
             when(entry[4], lambda: forward_copy(entry).start())
 
-    def clear(entry):
-        level, slot = entry[0], entry[2]
-        for ref in (in_slot(level, slot), at_slot(rxbox[level], level, slot)):
-            ref[...] = jnp.zeros(ref.shape, BF16)
-
+    def clear(ref):
+        ref[...] = jnp.zeros(ref.shape, BF16)
+
+    for entry in outward:
+        if entry[6] is not None:
+            when(jnp.logical_not(entry[6]), lambda: clear(in_slot(entry[0], entry[2])))
     for entry in peers:
         if entry[4] is not None:
-            when(jnp.logical_not(entry[4]), lambda: clear(entry))
+            when(
+                jnp.logical_not(entry[4]),
+                lambda: clear(at_slot(rxbox[entry[0]], entry[0], entry[2])),
+            )
 
     loads[2].wait()
     loads[3].wait()
@@ -255,7 +318,7 @@
         return jnp.where(bad, NEG, 0.0).astype(F32)
 
     no_prev, no_next = off_if(s == 0), off_if(s == seq_count - 1)
-    a, y = lax.div(s, 2), lax.div(s, 4)
+    a = lax.div(s, 2)
 
     def thirds(first, second, last):
         return jnp.where(lane < 128, first, jnp.where(lane < 256, second, last))[:1]
@@ -304,8 +367,8 @@
     forward(0, 1)
     forward(0, 2)
     for level in SEND_ORDER:
-        for entry in at_level(level):
-            when(entry[4], lambda: forward_arrival(entry))
+        for entry in out_level(level):
+            when(entry[6], lambda: forward_arrival(entry))
         if level == 0:
             in1[pl.ds(0, 64), :] = halve(kv0[pl.ds(0, BLOCK), :].astype(F32)).astype(BF16)
             in1[pl.ds(448, 64), :] = halve(kv0[pl.ds(640, BLOCK), :].astype(F32)).astype(BF16)
@@ -351,8 +414,12 @@
     def start_back(level):
         for entry in peers:
             if entry[0] == level:
-                when(entry[4], lambda: back_copy(entry).start())
-
+                when(entry[6], lambda: back_copy(entry).start())
+
+    for level in (4, 3):
+        for part, lanes in sides(backward(level)):
+            outbox[level][:, lanes] = part.astype(BF16)
+        start_back(level)
     for part, lanes in sides(backward(1, 0)):
         acc1[pl.ds(0, 384), lanes] = part
     for part, lanes in sides(backward(1, 1)):
@@ -371,7 +438,7 @@
         fold = 0.5 * expand(edge[pl.ds(64, 64), lanes], 1)
         bk0[pl.ds(128, 128), lanes] = (part[256:] + fold).astype(BF16)
     start_back(0)
-    for level in BACK_ORDER:
+    for level in (2,):
         for part, lanes in sides(backward(level)):
             outbox[level][:, lanes] = part.astype(BF16)
         start_back(level)
@@ -413,9 +480,21 @@
         for l in (3, 2, 1, 0):
             total = dq[pl.ds(OFF[l] + (BLOCK >> l) * b, BLOCK >> l), :] + 0.5 * expand(total, 1)
         oq[pl.ds(BLOCK * b, BLOCK), :] = dot(unperm, total.astype(BF16)).astype(BF16)
-    for j in range(1, head_count):
+    for j in FAR_FIRST:
         out_copy(0, oq, gq_ref, j).start()
     keep(oq, gq_ref)
+
+    for entry in at_level(4) + at_level(3):
+        when(entry[4], lambda: back_arrival(entry))
+    sum4 = rx4[pl.ds(0, BLOCK), :].astype(F32) + rx4[pl.ds(BLOCK, BLOCK), :].astype(F32)
+    panel[...] = 0.5 * expand(sum4, 1)
+    near_rows = pl.ds(pl.multiple_of(right * BLOCK, BLOCK), BLOCK)
+    far_rows = pl.ds(pl.multiple_of((1 - right) * BLOCK, BLOCK), BLOCK)
+    panel[near_rows, :] += rx3[pl.ds(0, BLOCK), :].astype(F32) + rx3[pl.ds(BLOCK, BLOCK), :].astype(F32)
+    panel[far_rows, :] += rx3[pl.ds(2 * BLOCK, BLOCK), :].astype(F32)
+    cots[...] = panel[...].astype(BF16)
+    for d in (2, 1, 3):
+        piece_back(d).start()
 
     for entry in at_level(1) + at_level(0):
         when(entry[4], lambda: back_arrival(entry))
@@ -433,16 +512,19 @@
         done = dot(unperm, total.astype(BF16)).astype(BF16)
         ok[pl.ds(BLOCK * b, BLOCK), :] = done[:, :BLOCK]
         ov[pl.ds(BLOCK * b, BLOCK), :] = done[:, BLOCK:]
-    for j in range(1, head_count):
+    for j in FAR_FIRST:
         out_copy(1, ok, gk_ref, j).start()
         out_copy(2, ov, gv_ref, j).start()
     keep(ok, gk_ref)
     keep(ov, gv_ref)
 
-    for entry in at_level(2) + at_level(3) + at_level(4):
+    for entry in at_level(2):
         when(entry[4], lambda: back_arrival(entry))
-    sum4 = sum(rx4[pl.ds(32 * i, 32), :].astype(F32) for i in range(8))
-    sum3 = sum(rx3[pl.ds(64 * i, 64), :].astype(F32) for i in range(6)) + 0.5 * expand(sum4, 1)
+    sum3 = panel[pl.ds(pl.multiple_of(x * 64, 64), 64), :]
+    for d in (1, 2, 3):
+        row_arrival(parts, back_send, back_recv, d)
+        frm = lax.rem(x + d, 4)
+        sum3 = sum3 + parts[pl.ds(pl.multiple_of(frm * 64, 64), 64), :].astype(F32)
     sum2 = sum(rx2[pl.ds(128 * i, 128), :].astype(F32) for i in range(3)) + 0.5 * expand(sum3, 1)
     r64, c64 = row[:64, :64], col[:64, :64]
     nth = 8 * (r64 >> 4) + (r64 & 7)
@@ -453,11 +535,15 @@
         part = sum2[32 * b : 32 * b + 32]
         part = jnp.concatenate([part[:, :BLOCK], part[:, BLOCK:]], axis=0).astype(BF16)
         oc[pl.ds(64 * b, 64), :] = dot(pick, part).astype(BF16)
-    for j in range(1, head_count):
+    for j in FAR_FIRST:
         out_copy(3, oc, coarse, j).start()
     keep(oc, coarse)
     for entry in peers:
-        when(entry[4], lambda: (forward_copy(entry).wait_send(), back_copy(entry).wait_send()) and None)
+        when(entry[6], lambda: back_copy(entry).wait_send())
+    for entry in outward:
+        when(entry[4], lambda: forward_copy(entry).wait_send())
+    for d in (1, 2, 3):
+        piece_back(d).wait_send()
     for index, src, dst in ((0, oq, gq_ref), (1, ok, gk_ref), (2, ov, gv_ref), (3, oc, coarse)):
         for j in range(1, head_count):
             out_copy(index, src, dst, j).wait_send()
@@ -508,11 +594,12 @@
                 wide(512, F32), wide(384, F32), wide(128, F32),
                 wide(256), wide(512), wide(384), wide(384), wide(256),
                 wide(256), wide(384), wide(384), wide(384), wide(256),
+                wide(256, F32), wide(256), wide(256),
                 *[pltpu.VMEM((rows, width), BF16) for _ in range(3)],
                 pltpu.VMEM((256, BLOCK), BF16), pltpu.VMEM((16, width * head_count), BF16),
                 *[pltpu.VMEM((rows, width), BF16) for _ in range(4)],
                 sems((4,)),
-                sems((SLOTS,)), sems((SLOTS,)), sems((SLOTS,)), sems((SLOTS,)),
+                sems((OUT_SLOTS,)), sems((OUT_SLOTS,)), sems((SLOTS,)), sems((SLOTS,)),
                 sems((4, head_count)), sems((4, head_count)),
             ],
             compiler_params=pltpu.CompilerParams(

time: 44.8 us -> 44.7 us (level)
  no operation moved by 1% of the time
where the time goes in v3:
time: 44.7 us; the launch traced here: 44.6 us
  Pallas kernels  43.9 us (98%)
  between operations  0.64 us (1%)
    pallas_call x1, Pallas kernels, step(): pl.pallas_call(functools.partial(kernel, seq_count, head_count), out_shap...  43.1 us

profile of v3, /device:TPU:1, one launch (start us, length us, event | category | flops | bytes accessed | tf_op | source)
XLA Modules:
  0.0 44.6 jit_solution(10951174307266993105)
XLA Ops:
  0.6 43.1 %shard_map.75 = (bf16[512,128]{1,0:T(8,128)(2,1)S(1)}, bf16[32,2048]{1,0:T(8,128)(2,1)S(1)}, bf16[32,2048]{1,0:T(8,128)(2,1)S(1)}, bf16[32,2048]{1,0:T(8,128)(2,1)S(1)}) custom-call(bf16[512,128]{1,0:T(8,128)(2,1)} %q_hbm.1, bf16[512,128]{1,0:T(8,128)(2,1)} %k_hbm.1, bf16[512,128]{1,0:T(8,128)(2,1)} %v_hbm.1, bf16[512,128]{1,0:T(8,128)(2,1)} %g_hbm.1), custom_call_target="tpu_custom_call" | custom-call | tf_op jit(solution)/shard_map/pallas_call | solution.py:584
  43.8 0.8 %shard_map.76 = (bf16[512,128]{1,0:T(8,128)(2,1)}, bf16[32,2048]{1,0:T(8,128)(2,1)}, bf16[32,2048]{1,0:T(8,128)(2,1)}, bf16[32,2048]{1,0:T(8,128)(2,1)}) custom-call(bf16[512,128]{1,0:T(8,128)(2,1)S(1)} %get-tuple-element.8.a, bf16[32,2048]{1,0:T(8,128)(2,1)S(1)} %get-tuple-element.9.b, bf16[32,2048]{1,0:T(8,128)(2,1)S(1)} %get-tuple-element.10.c, ...), custom_call_target="tpu_custom_call" | custom-call | tf_op jit(solution)/shard_map/pallas_call | solution.py:609

commit v4 on v3

--- a/solution.py
+++ b/solution.py
@@ -25,6 +25,7 @@
 ROWS = (128, 192, 128, 128, 128)
 
 SEND_ORDER = (0, 1, 4, 3, 2)
+FIRST_FAR = 4
 FAR_FIRST = (8, 7, 9, 6, 10, 5, 11, 4, 12, 3, 13, 2, 14, 1, 15)
 NN = (((1,), (0,)), ((), ()))
 NT = (((1,), (1,)), ((), ()))
@@ -127,7 +128,7 @@
     qs, go, ee, pk, tot, sm, gg, dd, dq,
     acc0, acc1, edge, bk0, bk1, bk2, bk3, bk4, rx0, rx1, rx2, rx3, rx4,
     panel, cots, parts, oq, ok, ov, oc, coarse, q_ref, k_ref, v_ref, g_ref, load_sem,
-    send_sem, recv_sem, back_send, back_recv, out_send, out_recv,
+    send_sem, recv_sem, back_send, back_recv, out_send, out_recv, row_sem, chip_sem, core_sem,
 ):
     s, h = lax.axis_index("seq"), lax.axis_index("head")
     barrier = pltpu.get_barrier_semaphore()
@@ -140,14 +141,19 @@
     for load in loads:
         load.start()
     y, x = lax.div(s, 4), lax.rem(s, 4)
-    for j in range(1, seq_count):
-        pl.semaphore_signal(
-            barrier, inc=1, device_id={"seq": lax.rem(s + j, seq_count)}, device_id_type=MESH
-        )
-    for j in range(1, head_count):
-        pl.semaphore_signal(
-            barrier, inc=1, device_id={"head": lax.rem(h + j, head_count)}, device_id_type=MESH
-        )
+    row_mates = [y * 4 + lax.rem(x + d, 4) for d in (1, 2, 3)]
+    near = [lax.rem(s + seq_count + d, seq_count) for d in (-1, 1)] + row_mates
+    near += [lax.rem(s + 4 * d, seq_count) for d in (1, 2, 3)]
+    core = h + 1 - 2 * lax.rem(h, 2)
+    two_away = [lax.rem(h + d, head_count) for d in (4, head_count - 4)]
+    near_head = [core] + two_away + [lax.rem(h + d, head_count) for d in (2, head_count - 2)]
+
+    def tell(sem, axis, peers):
+        for peer in peers:
+            pl.semaphore_signal(sem, inc=1, device_id={axis: peer}, device_id_type=MESH)
+
+    tell(barrier, "seq", near)
+    tell(barrier, "head", near_head)
 
     row = lax.broadcasted_iota(jnp.int32, (BLOCK, BLOCK), 0)
     col = lax.broadcasted_iota(jnp.int32, (BLOCK, BLOCK), 1)
@@ -170,7 +176,9 @@
         tops.append(halve(m3))
     kv4[...] = jnp.concatenate(tops, axis=0).astype(BF16)
 
-    pl.semaphore_wait(barrier, seq_count - 1 + head_count - 1)
+    pl.semaphore_wait(barrier, len(near) + len(near_head))
+    tell(row_sem, "seq", row_mates)
+    tell(chip_sem, "head", two_away)
 
     peers = peers_of(s, seq_count)
     outward = [entry for entry in peers if entry[0] < 3] + direct_of(s, seq_count)
@@ -277,6 +285,8 @@
         return [entry for entry in outward if entry[0] == level]
 
     for level in SEND_ORDER:
+        if level == FIRST_FAR:
+            pl.semaphore_wait(row_sem, len(row_mates))
         for entry in out_level(level):
             when(entry[4], lambda: forward_copy(entry).start())
 
@@ -379,6 +389,9 @@
             forward(1, 1)
         else:
             forward(level)
+
+    pl.semaphore_wait(chip_sem, len(two_away))
+    tell(core_sem, "head", [core])
 
     for b in range(4):
         where = [pl.ds(OFF[l] + (BLOCK >> l) * b, BLOCK >> l) for l in range(5)]
@@ -475,6 +488,7 @@
             pl.ds(pl.multiple_of(h * dst.shape[0], dst.shape[0]), dst.shape[0]), :
         ]
 
+    pl.semaphore_wait(core_sem, 1)
     for b in range(4):
         total = dq[pl.ds(OFF[4] + 8 * b, 8), :]
         for l in (3, 2, 1, 0):
@@ -601,6 +615,7 @@
                 sems((4,)),
                 sems((OUT_SLOTS,)), sems((OUT_SLOTS,)), sems((SLOTS,)), sems((SLOTS,)),
                 sems((4, head_count)), sems((4, head_count)),
+                *[pltpu.SemaphoreType.REGULAR for _ in range(3)],
             ],
             compiler_params=pltpu.CompilerParams(
                 collective_id=0, has_side_effects=True, vmem_limit_bytes=56000000

time: 44.7 us -> 42.4 us (0.949)
  Pallas kernels: 43.9 us -> 41.2 us
    pallas_call x1, Pallas kernels: 43.1 us -> 40.4 us  [step(): pl.pallas_call(functools.partial(kernel, seq_count, head_count), out_shap...]
where the time goes in v4:
time: 42.4 us; the launch traced here: 41.9 us
  Pallas kernels  41.2 us (97%)
  between operations  0.64 us (2%)
    pallas_call x1, Pallas kernels, step(): pl.pallas_call(functools.partial(kernel, seq_count, head_count), out_shap...  40.4 us

profile of v4, /device:TPU:1, one launch (start us, length us, event | category | flops | bytes accessed | tf_op | source)
XLA Modules:
  0.0 41.9 jit_solution(5099784620607533455)
XLA Ops:
  0.6 40.4 %shard_map.75 = (bf16[512,128]{1,0:T(8,128)(2,1)S(1)}, bf16[32,2048]{1,0:T(8,128)(2,1)S(1)}, bf16[32,2048]{1,0:T(8,128)(2,1)S(1)}, bf16[32,2048]{1,0:T(8,128)(2,1)S(1)}) custom-call(bf16[512,128]{1,0:T(8,128)(2,1)} %q_hbm.1, bf16[512,128]{1,0:T(8,128)(2,1)} %k_hbm.1, bf16[512,128]{1,0:T(8,128)(2,1)} %v_hbm.1, bf16[512,128]{1,0:T(8,128)(2,1)} %g_hbm.1), custom_call_target="tpu_custom_call" | custom-call | tf_op jit(solution)/shard_map/pallas_call | solution.py:598
  41.0 0.8 %shard_map.76 = (bf16[512,128]{1,0:T(8,128)(2,1)}, bf16[32,2048]{1,0:T(8,128)(2,1)}, bf16[32,2048]{1,0:T(8,128)(2,1)}, bf16[32,2048]{1,0:T(8,128)(2,1)}) custom-call(bf16[512,128]{1,0:T(8,128)(2,1)S(1)} %get-tuple-element.8.a, bf16[32,2048]{1,0:T(8,128)(2,1)S(1)} %get-tuple-element.9.b, bf16[32,2048]{1,0:T(8,128)(2,1)S(1)} %get-tuple-element.10.c, ...), custom_call_target="tpu_custom_call" | custom-call | tf_op jit(solution)/shard_map/pallas_call | solution.py:624

commit v5 on v4

--- a/solution.py
+++ b/solution.py
@@ -123,11 +123,11 @@
 def kernel(
     seq_count, head_count,
     q_hbm, k_hbm, v_hbm, g_hbm,
-    att_ref, gq_ref, gk_ref, gv_ref,
+    att_ref, gq_ref, gk_ref, gv_ref, coarse,
     kv0, kv1, kv2, kv3, kv4, in1, in2, in3, in4,
     qs, go, ee, pk, tot, sm, gg, dd, dq,
     acc0, acc1, edge, bk0, bk1, bk2, bk3, bk4, rx0, rx1, rx2, rx3, rx4,
-    panel, cots, parts, oq, ok, ov, oc, coarse, q_ref, k_ref, v_ref, g_ref, load_sem,
+    panel, cots, parts, oq, ok, ov, oc, q_ref, k_ref, v_ref, g_ref, load_sem,
     send_sem, recv_sem, back_send, back_recv, out_send, out_recv, row_sem, chip_sem, core_sem,
 ):
     s, h = lax.axis_index("seq"), lax.axis_index("head")
@@ -562,20 +562,24 @@
         for j in range(1, head_count):
             out_copy(index, src, dst, j).wait_send()
             out_arrival(index, dst, j)
-    r16, c16 = row[:64, :16], col[:64, :16]
+
+
+def write_out(a, b, c, d, coarse, a_out, b_out, c_out, d_out, keys, values, sem):
+    copies = [
+        pltpu.make_async_copy(src, dst, sem.at[i])
+        for i, (src, dst) in enumerate(((a, a_out), (b, b_out), (keys, c_out), (values, d_out)))
+    ]
+    copies[0].start()
+    copies[1].start()
+    chunk = c.shape[0]
+    r16 = lax.broadcasted_iota(jnp.int32, (2 * chunk, 16), 0)
+    c16 = lax.broadcasted_iota(jnp.int32, (2 * chunk, 16), 1)
     spread = jnp.where(c16 == 8 * (r16 >> 5) + ((r16 & 31) >> 2), 0.25, 0.0).astype(BF16)
     more = dot(spread, coarse[...])
-    gk_ref[...] = (gk_ref[...].astype(F32) + more[:chunk]).astype(BF16)
-    gv_ref[...] = (gv_ref[...].astype(F32) + more[chunk:]).astype(BF16)
-
-
-def write_out(a, b, c, d, a_out, b_out, c_out, d_out, sem):
-    copies = [
-        pltpu.make_async_copy(src, dst, sem.at[i])
-        for i, (src, dst) in enumerate(((a, a_out), (b, b_out), (c, c_out), (d, d_out)))
-    ]
-    for copy in copies:
-        copy.start()
+    keys[...] = (c[...].astype(F32) + more[:chunk]).astype(BF16)
+    copies[2].start()
+    values[...] = (d[...].astype(F32) + more[chunk:]).astype(BF16)
+    copies[3].start()
     for copy in copies:
         copy.wait()
 
@@ -597,9 +601,12 @@
         sems = pltpu.SemaphoreType.DMA
         results = pl.pallas_call(
             functools.partial(kernel, seq_count, head_count),
-            out_shape=(jax.ShapeDtypeStruct((rows, width), BF16), grad, grad, grad),
+            out_shape=(
+                jax.ShapeDtypeStruct((rows, width), BF16), grad, grad, grad,
+                jax.ShapeDtypeStruct((16, width * head_count), BF16),
+            ),
             in_specs=[pl.BlockSpec(memory_space=pltpu.HBM)] * 4,
-            out_specs=(vmem,) * 4,
+            out_specs=(vmem,) * 5,
             scratch_shapes=[
                 wide(768), wide(256), wide(128), wide(64), wide(32),
                 wide(512), wide(384), wide(384), wide(256),
@@ -610,7 +617,7 @@
                 wide(256), wide(384), wide(384), wide(384), wide(256),
                 wide(256, F32), wide(256), wide(256),
                 *[pltpu.VMEM((rows, width), BF16) for _ in range(3)],
-                pltpu.VMEM((256, BLOCK), BF16), pltpu.VMEM((16, width * head_count), BF16),
+                pltpu.VMEM((256, BLOCK), BF16),
                 *[pltpu.VMEM((rows, width), BF16) for _ in range(4)],
                 sems((4,)),
                 sems((OUT_SLOTS,)), sems((OUT_SLOTS,)), sems((SLOTS,)), sems((SLOTS,)),
@@ -618,15 +625,15 @@
                 *[pltpu.SemaphoreType.REGULAR for _ in range(3)],
             ],
             compiler_params=pltpu.CompilerParams(
-                collective_id=0, has_side_effects=True, vmem_limit_bytes=56000000
+                collective_id=0, has_side_effects=True, vmem_limit_bytes=55900000
             ),
         )(queries, keys, values, grad_out)
         return pl.pallas_call(
             write_out,
-            out_shape=tuple(jax.ShapeDtypeStruct(r.shape, r.dtype) for r in results),
-            in_specs=[vmem] * 4,
+            out_shape=tuple(jax.ShapeDtypeStruct(r.shape, r.dtype) for r in results[:4]),
+            in_specs=[vmem] * 5,
             out_specs=(pl.BlockSpec(memory_space=pltpu.HBM),) * 4,
-            scratch_shapes=[sems((4,))],
+            scratch_shapes=[pltpu.VMEM(grad.shape, BF16), pltpu.VMEM(grad.shape, BF16), sems((4,))],
             compiler_params=pltpu.CompilerParams(vmem_limit_bytes=1024 * 1024),
         )(*results)
 

time: 42.4 us -> 42.3 us (level)
  no operation moved by 1% of the time
where the time goes in v5:
time: 42.3 us; the launch traced here: 41.8 us
  Pallas kernels  41.1 us (97%)
  between operations  0.64 us (2%)
    pallas_call x1, Pallas kernels, step(): pl.pallas_call(functools.partial(kernel, seq_count, head_count), out_shap...  40.2 us
    pallas_call x1, Pallas kernels, step(): pl.pallas_call(write_out, out_shape=tuple((jax.ShapeDtypeStruct(r.shape,...  0.94 us

profile of v5, /device:TPU:1, one launch (start us, length us, event | category | flops | bytes accessed | tf_op | source)
XLA Modules:
  0.0 41.8 jit_solution(807626518844809230)
XLA Ops:
  0.6 40.2 %shard_map.75 = (bf16[512,128]{1,0:T(8,128)(2,1)S(1)}, bf16[32,2048]{1,0:T(8,128)(2,1)S(1)}, bf16[32,2048]{1,0:T(8,128)(2,1)S(1)}, bf16[32,2048]{1,0:T(8,128)(2,1)S(1)}, bf16[16,2048]{1,0:T(8,128)(2,1)S(1)}) custom-call(bf16[512,128]{1,0:T(8,128)(2,1)} %q_hbm.1, bf16[512,128]{1,0:T(8,128)(2,1)} %k_hbm.1, bf16[512,128]{1,0:T(8,128)(2,1)} %v_hbm.1, ...), custom_call_target="tpu_custom_call" | custom-call | tf_op jit(solution)/shard_map/pallas_call | solution.py:602
  40.8 0.9 %shard_map.76 = (bf16[512,128]{1,0:T(8,128)(2,1)}, bf16[32,2048]{1,0:T(8,128)(2,1)}, bf16[32,2048]{1,0:T(8,128)(2,1)}, bf16[32,2048]{1,0:T(8,128)(2,1)}) custom-call(bf16[512,128]{1,0:T(8,128)(2,1)S(1)} %get-tuple-element.9.a, bf16[32,2048]{1,0:T(8,128)(2,1)S(1)} %get-tuple-element.10.b, bf16[32,2048]{1,0:T(8,128)(2,1)S(1)} %get-tuple-element.11.c, ...), custom_call_target="tpu_custom_call" | custom-call | tf_op jit(solution)/shard_map/pallas_call | solution.py:631

commit v6 on v4

--- a/solution.py
+++ b/solution.py
@@ -25,7 +25,6 @@
 ROWS = (128, 192, 128, 128, 128)
 
 SEND_ORDER = (0, 1, 4, 3, 2)
-FIRST_FAR = 4
 FAR_FIRST = (8, 7, 9, 6, 10, 5, 11, 4, 12, 3, 13, 2, 14, 1, 15)
 NN = (((1,), (0,)), ((), ()))
 NT = (((1,), (1,)), ((), ()))
@@ -127,7 +126,7 @@
     kv0, kv1, kv2, kv3, kv4, in1, in2, in3, in4,
     qs, go, ee, pk, tot, sm, gg, dd, dq,
     acc0, acc1, edge, bk0, bk1, bk2, bk3, bk4, rx0, rx1, rx2, rx3, rx4,
-    panel, cots, parts, oq, ok, ov, oc, coarse, q_ref, k_ref, v_ref, g_ref, load_sem,
+    panel, cots, parts, oa, oq, ok, ov, oc, coarse, q_ref, k_ref, v_ref, g_ref, load_sem,
     send_sem, recv_sem, back_send, back_recv, out_send, out_recv, row_sem, chip_sem, core_sem,
 ):
     s, h = lax.axis_index("seq"), lax.axis_index("head")
@@ -284,9 +283,7 @@
     def out_level(level):
         return [entry for entry in outward if entry[0] == level]
 
-    for level in SEND_ORDER:
-        if level == FIRST_FAR:
-            pl.semaphore_wait(row_sem, len(row_mates))
+    for level in (0, 1):
         for entry in out_level(level):
             when(entry[4], lambda: forward_copy(entry).start())
 
@@ -321,6 +318,11 @@
         tops.append(halve(m3))
     qs[pl.ds(OFF[4], 32), :] = jnp.concatenate(tops, axis=0).astype(BF16)
 
+    pl.semaphore_wait(row_sem, len(row_mates))
+    for level in (4, 3, 2):
+        for entry in out_level(level):
+            when(entry[4], lambda: forward_copy(entry).start())
+
     scale = BLOCK ** (-0.5)
     lane = lax.broadcasted_iota(jnp.int32, (8, 384), 1)
 
@@ -402,7 +404,7 @@
         num = sum(factors[l] * expand(sm[where[l], :], l) for l in range(5))
         inverse = 1.0 / den
         out = num * inverse
-        att_ref[pl.ds(BLOCK * b, BLOCK), :] = dot(unperm, out.astype(BF16)).astype(BF16)
+        oa[pl.ds(BLOCK * b, BLOCK), :] = out.astype(BF16)
         cot = go[pl.ds(BLOCK * b, BLOCK), :]
         delta = jnp.broadcast_to(jnp.sum(cot * out, axis=1, keepdims=True), (BLOCK, BLOCK))
         cot, delta = cot * inverse, delta * inverse
@@ -497,6 +499,9 @@
     for j in FAR_FIRST:
         out_copy(0, oq, gq_ref, j).start()
     keep(oq, gq_ref)
+    for b in range(4):
+        rows = pl.ds(BLOCK * b, BLOCK)
+        att_ref[rows, :] = dot(unperm, oa[rows, :]).astype(BF16)
 
     for entry in at_level(4) + at_level(3):
         when(entry[4], lambda: back_arrival(entry))
@@ -609,7 +614,7 @@
                 wide(256), wide(512), wide(384), wide(384), wide(256),
                 wide(256), wide(384), wide(384), wide(384), wide(256),
                 wide(256, F32), wide(256), wide(256),
-                *[pltpu.VMEM((rows, width), BF16) for _ in range(3)],
+                *[pltpu.VMEM((rows, width), BF16) for _ in range(4)],
                 pltpu.VMEM((256, BLOCK), BF16), pltpu.VMEM((16, width * head_count), BF16),
                 *[pltpu.VMEM((rows, width), BF16) for _ in range(4)],
                 sems((4,)),

time: 42.4 us -> 42.4 us (level)
  no operation moved by 1% of the time
where the time goes in v6:
time: 42.4 us; the launch traced here: 41.8 us
  Pallas kernels  41.2 us (97%)
  between operations  0.64 us (2%)
    pallas_call x1, Pallas kernels, step(): pl.pallas_call(functools.partial(kernel, seq_count, head_count), out_shap...  40.4 us

profile of v6, /device:TPU:1, one launch (start us, length us, event | category | flops | bytes accessed | tf_op | source)
XLA Modules:
  0.0 41.8 jit_solution(9493383970806807467)
XLA Ops:
  0.6 40.4 %shard_map.75 = (bf16[512,128]{1,0:T(8,128)(2,1)S(1)}, bf16[32,2048]{1,0:T(8,128)(2,1)S(1)}, bf16[32,2048]{1,0:T(8,128)(2,1)S(1)}, bf16[32,2048]{1,0:T(8,128)(2,1)S(1)}) custom-call(bf16[512,128]{1,0:T(8,128)(2,1)} %q_hbm.1, bf16[512,128]{1,0:T(8,128)(2,1)} %k_hbm.1, bf16[512,128]{1,0:T(8,128)(2,1)} %v_hbm.1, bf16[512,128]{1,0:T(8,128)(2,1)} %g_hbm.1), custom_call_target="tpu_custom_call" | custom-call | tf_op jit(solution)/shard_map/pallas_call | solution.py:603
  41.0 0.8 %shard_map.76 = (bf16[512,128]{1,0:T(8,128)(2,1)}, bf16[32,2048]{1,0:T(8,128)(2,1)}, bf16[32,2048]{1,0:T(8,128)(2,1)}, bf16[32,2048]{1,0:T(8,128)(2,1)}) custom-call(bf16[512,128]{1,0:T(8,128)(2,1)S(1)} %get-tuple-element.8.a, bf16[32,2048]{1,0:T(8,128)(2,1)S(1)} %get-tuple-element.9.b, bf16[32,2048]{1,0:T(8,128)(2,1)S(1)} %get-tuple-element.10.c, ...), custom_call_target="tpu_custom_call" | custom-call | tf_op jit(solution)/shard_map/pallas_call | solution.py:629
